TPU v7x, 32 devices: a whole 2x2x4 slice. The times are simulated.
32 devices in a mesh: pole: 2 (over x), row: 8 (over z, y), col: 2 (over core).
Axes of the slice: x: 2, y: 2, z: 4, core: 2. Of those that a mesh axis runs over, the one named last changes fastest.
Arguments:
- panel: bfloat16 [4, 8, 2, 512, 128], P(('pole', 'col'), None, None, 'row'), parts along dimension 0, may hold values from -6 to 6
- tiles: bfloat16 [352, 2, 512, 512], P(('pole', 'row', 'col')), parts along dimension 0, may hold values from -0.078125 to 0.078125
- tile_slot: int32 [352], P(('pole', 'row', 'col')), parts along dimension 0, may hold values from 0 to 1
- tile_col: int32 [352], P(('pole', 'row', 'col')), parts along dimension 0, may hold values from 0 to 7
- pole_weight: float32 [4], P('pole'), parts along dimension 0, may hold values from -4 to 4
- box_orbitals: int32 [64, 256], P(('pole', 'row', 'col')), parts along dimension 0, may hold values from 0 to 8191, as said below
- box_basis: bfloat16 [64, 256, 512], P(('pole', 'row', 'col')), parts along dimension 0, may hold values from -0.375 to 0.375
- supernode_basis: bfloat16 [64, 128, 512], P(('pole', 'row', 'col')), parts along dimension 0, may hold values from -0.5 to 0.5
Outputs:
- inverse_column: float32 [32, 2, 512, 128], P(('pole', 'row'), None, 'col'), parts along dimension 0
- density: float32 [64, 512], P(('pole', 'row', 'col')), parts along dimension 0
There are 2 independent parts, one for each index of `pole`. A program takes and returns all parts, laid end to end along the dimension named above; each array names one. Nothing has to cross between parts.
Inputs may be any that keep to these rules, and one draw needn't show every extreme that they name: `box_orbitals`: let a row g be held by device r * 2 + c where r = (g // 512) // 2 and c = (g % 512) // (512 // 2). The 2 boxes of one device take at most 64 rows (counted with repeats) held by any one device, and exactly 64 from some device.
All inputs are finite; a program needn't handle non-finite values.
Results may differ from a plain program's by a relative error of at most 0.0029.
Values may be sent and summed in bfloat16 or wider, within the bound.
A program may use at most 64 MiB of HBM per device.

v0:
```python
import functools

import jax
import jax.numpy as jnp
from jax import lax
from jax.experimental import pallas as pl
from jax.experimental.pallas import tpu as pltpu
from jax.sharding import PartitionSpec as P

BR_DEV = 2
MESH = pl.DeviceIdType.MESH


def log2(value):
    assert value & (value - 1) == 0
    return value.bit_length() - 1


def kernel(
    rows, cols, slot_ref, tcol_ref, weight_ref, panel, tiles, orbitals, basis, super_basis,
    inv_ref, density_ref, *scratch,
):
    lanes_y = 2
    depth_z = rows // lanes_y
    chunk_count = 2 * depth_z - 1
    chunks = scratch[:chunk_count]
    (tile_buf, basis_buf, super_buf, orb_buf, acc, half_in, pick_hot, basis_hot, send_rows, recv_rows,
     local_sem, z_send, z_recv, y_send, y_recv, x_send, x_recv, col_sem, orb_send, orb_recv, row_send, row_recv) = scratch[chunk_count:]
    peers = rows * cols
    r = lax.axis_index("row")
    c = lax.axis_index("col")
    me = r * cols + c
    z = r // lanes_y
    y = r % lanes_y
    shard_rows = panel.shape[3]
    width = panel.shape[4]
    tile_count = tiles.shape[0]
    block = tiles.shape[2]
    half = block // cols
    pair = lanes_y * shard_rows
    boxes, orbs = orbitals.shape
    capacity = send_rows.shape[1]
    pieces = z_send.shape[2]
    late = pieces // 2
    step = panel.shape[1] // pieces

    def spot(index):
        return {"row": index // cols, "col": index % cols}

    loads = [
        pltpu.make_async_copy(panel.at[0], chunks[0].at[y], local_sem.at[0]),
        pltpu.make_async_copy(tiles, tile_buf, local_sem.at[1]),
        pltpu.make_async_copy(basis, basis_buf, local_sem.at[2]),
        pltpu.make_async_copy(super_basis, super_buf, local_sem.at[3]),
        pltpu.make_async_copy(orbitals, orb_buf.at[me], local_sem.at[4]),
    ]
    for load in loads:
        load.start()
    acc[...] = jnp.zeros_like(acc)

    barrier = pltpu.get_barrier_semaphore()
    for k in range(1, peers):
        pl.semaphore_signal(barrier, inc=1, device_id=spot((me + k) % peers), device_id_type=MESH)
    pl.semaphore_wait(barrier, peers - 1)

    def up(d):
        return d

    def down(d):
        return d if d == 0 else depth_z - 1 + d

    idents = {"up": up, "down": down}
    sides = {"up": 0, "down": 1}
    other = r + 1 - 2 * y
    partner = r + lanes_y - 2 * lanes_y * (z % 2)

    def has(kind, d):
        return z - d >= 0 if kind == "up" else z + d < depth_z

    def can_send(kind):
        return z + 1 < depth_z if kind == "up" else z >= 1

    def from_partner(kind):
        return z % 2 == 1 if kind == "up" else z % 2 == 0

    def piece(ref, h):
        return ref.at[pl.ds(h * step, step)]

    def z_copy(kind, d, h):
        side = sides[kind]
        src = panel.at[0] if d == 0 else chunks[idents[kind](d)].at[y]
        return pltpu.make_async_remote_copy(
            src_ref=piece(src, h), dst_ref=piece(chunks[idents[kind](d + 1)].at[y], h),
            send_sem=z_send.at[side, d, h], recv_sem=z_recv.at[side, d + 1, h],
            device_id={"row": r + lanes_y if kind == "up" else r - lanes_y}, device_id_type=MESH,
        )

    def z_arrival(kind, d, h):
        side = sides[kind]
        dst = piece(chunks[idents[kind](d)].at[y], h)
        return pltpu.make_async_remote_copy(
            src_ref=dst, dst_ref=dst, send_sem=z_send.at[side, d - 1, h], recv_sem=z_recv.at[side, d, h],
            device_id={"row": other}, device_id_type=MESH,
        )

    def y_copy(ident, h):
        src = panel.at[0] if ident == 0 else chunks[ident].at[y]
        return pltpu.make_async_remote_copy(
            src_ref=piece(src, h), dst_ref=piece(chunks[ident].at[y], h),
            send_sem=y_send.at[ident, h], recv_sem=y_recv.at[ident, h],
            device_id={"row": other}, device_id_type=MESH,
        )

    def y_arrival(ident, h):
        dst = piece(chunks[ident].at[1 - y], h)
        return pltpu.make_async_remote_copy(
            src_ref=dst, dst_ref=dst, send_sem=y_send.at[ident, h], recv_sem=y_recv.at[ident, h],
            device_id={"row": other}, device_id_type=MESH,
        )

    def extra_copy(kind, h):
        return pltpu.make_async_remote_copy(
            src_ref=piece(chunks[0].at[1 - y], h), dst_ref=piece(chunks[idents[kind](1)].at[1 - y], h),
            send_sem=x_send.at[h], recv_sem=x_recv.at[h],
            device_id={"row": partner}, device_id_type=MESH,
        )

    def extra_arrival(kind, h):
        dst = piece(chunks[idents[kind](1)].at[1 - y], h)
        return pltpu.make_async_remote_copy(
            src_ref=dst, dst_ref=dst, send_sem=x_send.at[h], recv_sem=x_recv.at[h],
            device_id={"row": partner}, device_id_type=MESH,
        )

    def each(low, high, body):
        def run(h, carry):
            body(h)
            return carry
        lax.fori_loop(low, high, run, 0)

    def y_forward(kind, d, h, act):
        ident = idents[kind](d)
        if d == 1:
            @pl.when(jnp.logical_or(jnp.logical_not(from_partner(kind)), h < late))
            def _():
                act(y_copy(ident, h))
        else:
            act(y_copy(ident, h))

    def chunk_ready(kind, d):
        ident = idents[kind](d)
        each(0, late if d == 1 else pieces, lambda h: y_arrival(ident, h).wait_recv())
        if d == 1:
            @pl.when(from_partner(kind))
            def _():
                each(late, pieces, lambda h: extra_arrival(kind, h).wait_recv())

            @pl.when(jnp.logical_not(from_partner(kind)))
            def _():
                each(late, pieces, lambda h: y_arrival(ident, h).wait_recv())

    def compute(ident, at_z, first, last, group=1):
        offset = pl.multiple_of(at_z * pair, pair)
        chunk = chunks[ident]

        def product(t):
            j = tcol_ref[t]
            left = jnp.concatenate(
                [tile_buf[t, 0, :, pl.ds(offset, pair)], tile_buf[t, 1, :, pl.ds(offset, pair)]], axis=1)
            parts = [chunk[k, j] for k in range(lanes_y)]
            real = jnp.concatenate([p[0] for p in parts], axis=0)
            imag = jnp.concatenate([p[1] for p in parts], axis=0)
            right = jnp.concatenate(
                [jnp.concatenate([real, imag], axis=1), jnp.concatenate([-imag, real], axis=1)], axis=0)
            return jnp.dot(left, right, preferred_element_type=jnp.float32)

        def several(start, count):
            values = [product(start + k) for k in range(count)]
            for s in range(BR_DEV):
                total = jnp.where(slot_ref[start] == s, values[0], 0.0)
                for k in range(1, count):
                    total = total + jnp.where(slot_ref[start + k] == s, values[k], 0.0)
                acc[s] += total

        if group == 1:
            each(first, last, lambda t: several(t, 1))
        else:
            for start in range(first, last, group):
                several(start, min(group, last - start))

    def at(kind, d):
        return z - d if kind == "up" else z + d

    orb_copies = []
    for k in range(1, peers):
        target = (me + k) % peers
        orb_copies.append(pltpu.make_async_remote_copy(
            src_ref=orbitals, dst_ref=orb_buf.at[me], send_sem=orb_send.at[k], recv_sem=orb_recv.at[k],
            device_id=spot(target), device_id_type=MESH,
        ))
        orb_copies[-1].start()

    def own_z(h):
        for kind in idents:
            @pl.when(can_send(kind))
            def _(kind=kind):
                z_copy(kind, 0, h).start()

    def own_piece(h):
        own_z(h)
        y_copy(0, (h + late) % pieces).start()

    each(0, pieces, own_piece)
    loads[0].wait()

    def prepare():
        for k in range(1, peers):
            origin = (me + peers - k) % peers
            dst = orb_buf.at[origin]
            pltpu.make_async_remote_copy(
                src_ref=orbitals, dst_ref=dst, send_sem=orb_send.at[k], recv_sem=orb_recv.at[k],
                device_id=spot(origin), device_id_type=MESH,
            ).wait()
        loads[4].wait()
        loads[2].wait()
        block_bits, half_bits = log2(block), log2(half)

        def split(g):
            row_block = g >> block_bits
            within = g & (block - 1)
            source = (row_block >> log2(BR_DEV)) * cols + (within >> half_bits)
            local = (row_block & (BR_DEV - 1)) * half + (within & (half - 1))
            return source, local

        before = lax.broadcasted_iota(jnp.int32, (orbs, orbs), 0)
        after = lax.broadcasted_iota(jnp.int32, (orbs, orbs), 1)
        upper = jnp.where(before <= after, 1.0, 0.0).astype(jnp.bfloat16)

        def ranks(masks):
            seen = jnp.zeros((masks[0].shape[0], 1), jnp.float32)
            result = []
            for mask in masks:
                counted = jnp.dot(mask.astype(jnp.bfloat16), upper, preferred_element_type=jnp.float32)
                result.append(counted - 1.0 + seen)
                seen = seen + jnp.sum(mask, axis=1, keepdims=True)
            return result

        asked = []
        for n in range(boxes):
            g = jnp.concatenate([orb_buf[q, n:n + 1, :] for q in range(peers)], axis=0)
            source, local = split(g)
            asked.append((jnp.where(source == me, 1.0, 0.0), local.astype(jnp.float32)))
        order = ranks([a[0] for a in asked])
        order = [jnp.where(a[0] > 0.5, o, -1.0) for a, o in zip(asked, order)]
        place = lax.broadcasted_iota(jnp.int32, (capacity, orbs), 0).astype(jnp.float32)
        row_id = lax.broadcasted_iota(jnp.int32, (capacity, BR_DEV * half), 1).astype(jnp.float32)
        for q in range(peers):
            found = jnp.zeros((capacity, 1), jnp.float32)
            for n in range(boxes):
                hit = place == order[n][q:q + 1]
                found = found + jnp.sum(jnp.where(hit, asked[n][1][q:q + 1] + 1.0, 0.0), axis=1, keepdims=True)
            pick_hot[q * capacity:(q + 1) * capacity, :] = jnp.where(
                row_id == found - 1.0, 1.0, 0.0).astype(jnp.bfloat16)

        masks = []
        peer_id = lax.broadcasted_iota(jnp.int32, (peers, orbs), 0)
        for n in range(boxes):
            source, _ = split(orb_buf[me, n:n + 1, :])
            masks.append(jnp.where(peer_id == source, 1.0, 0.0))
        order = ranks(masks)
        arrive = lax.broadcasted_iota(jnp.int32, (peers * capacity, orbs), 0).astype(jnp.float32)
        for n in range(boxes):
            position = jnp.sum(
                masks[n] * (order[n] + (peer_id * capacity).astype(jnp.float32)), axis=0, keepdims=True)
            hot = jnp.where(arrive == position, 1.0, 0.0).astype(jnp.bfloat16)
            basis_hot[n] = jnp.dot(hot, basis_buf[n], preferred_element_type=jnp.float32).astype(jnp.bfloat16)

    def send_extra(h):
        y_arrival(0, h).wait_recv()
        for kind in idents:
            @pl.when(jnp.logical_not(from_partner(kind)))
            def _(kind=kind):
                extra_copy(kind, h).start()

    each(late, pieces, send_extra)
    prepare()
    for d in range(1, depth_z):
        if d == 2:
            each(0, late, lambda h: y_arrival(0, h).wait_recv())
            loads[1].wait()
        if d >= 3:
            for kind in idents:
                @pl.when(has(kind, d - 2))
                def _(kind=kind):
                    chunk_ready(kind, d - 2)

        final = d >= 3 and d == depth_z - 1

        def arrive_piece(h, d=d, final=final, behind=2):
            for kind in idents:
                @pl.when(has(kind, d))
                def _(kind=kind):
                    z_arrival(kind, d, h).wait_recv()
                    if d < depth_z - 1:
                        @pl.when(can_send(kind))
                        def _():
                            z_copy(kind, d, h).start()
                    y_forward(kind, d, h, lambda copy: copy.start())
            first, last = h * tile_count // pieces, (h + 1) * tile_count // pieces
            if d == 2:
                compute(0, z, first, last)
            if final:
                done = h - (0 if behind == 2 else late)
                first, last = done * tile_count // late, (done + 1) * tile_count // late
            if d >= 3:
                for kind in idents:
                    @pl.when(has(kind, d if behind == 1 else d - 2))
                    def _(kind=kind):
                        compute(idents[kind](d - behind), at(kind, d - behind), first, last)

        if final:
            each(0, late, arrive_piece)
            for kind in idents:
                @pl.when(has(kind, d))
                def _(kind=kind, d=d):
                    chunk_ready(kind, d - 1)
            each(late, pieces, functools.partial(arrive_piece, behind=1))
        else:
            each(0, pieces, arrive_piece)
    if depth_z == 2:
        each(0, late, lambda h: y_arrival(0, h).wait_recv())
        loads[1].wait()
        compute(0, z, 0, tile_count)
    for d in range(max(depth_z - 2, 1), depth_z):
        for kind in idents:
            waiting = has(kind, d)
            if depth_z >= 4 and d == depth_z - 2:
                waiting = jnp.logical_and(waiting, jnp.logical_not(has(kind, d + 1)))

            @pl.when(waiting)
            def _(kind=kind, d=d):
                chunk_ready(kind, d)
                compute(idents[kind](d), at(kind, d), 0, tile_count, group=4)

    mine = pl.ds(pl.multiple_of(c * half, half), half)
    theirs = pl.ds(pl.multiple_of((1 - c) * half, half), half)
    swap = pltpu.make_async_remote_copy(
        src_ref=acc.at[:, theirs, :], dst_ref=half_in, send_sem=col_sem.at[0], recv_sem=col_sem.at[1],
        device_id={"col": 1 - c}, device_id_type=MESH,
    )
    swap.start()
    swap.wait_recv()
    density_rows = []
    for s in range(BR_DEV):
        column = -(acc[s, mine, :] + half_in[s])
        real, imag = column[:, :width], column[:, width:]
        density_rows.append((weight_ref[0] * imag + weight_ref[1] * real).astype(jnp.bfloat16))
    density_rows = jnp.concatenate(density_rows, axis=0)
    picked = jnp.dot(pick_hot[...], density_rows, preferred_element_type=jnp.float32).astype(jnp.bfloat16)
    send_rows[...] = picked.reshape(send_rows.shape)
    row_copies = []
    for k in range(1, peers):
        target = (me + k) % peers
        row_copies.append(pltpu.make_async_remote_copy(
            src_ref=send_rows.at[target], dst_ref=recv_rows.at[me],
            send_sem=row_send.at[k], recv_sem=row_recv.at[k],
            device_id=spot(target), device_id_type=MESH,
        ))
        row_copies[-1].start()
    recv_rows[me] = send_rows[me]
    for s in range(BR_DEV):
        column = -(acc[s, mine, :] + half_in[s])
        inv_ref[s, 0] = column[:, :width]
        inv_ref[s, 1] = column[:, width:]
    loads[3].wait()
    for k in range(1, peers):
        origin = (me + peers - k) % peers
        dst = recv_rows.at[origin]
        pltpu.make_async_remote_copy(
            src_ref=dst, dst_ref=dst, send_sem=row_send.at[k], recv_sem=row_recv.at[k],
            device_id=spot(origin), device_id_type=MESH,
        ).wait_recv()
    arrived = recv_rows[...].reshape(peers * capacity, width)
    for n in range(boxes):
        projected = lax.dot_general(
            arrived, basis_hot[n], (((0,), (0,)), ((), ())), preferred_element_type=jnp.float32)
        density_ref[n:n + 1, :] = jnp.sum(
            super_buf[n].astype(jnp.float32) * projected, axis=0, keepdims=True)

    def sent(h):
        y_copy(0, h).wait_send()
        for kind in idents:
            for d in range(depth_z - 1):
                @pl.when(jnp.logical_and(has(kind, d), can_send(kind)))
                def _(kind=kind, d=d):
                    z_copy(kind, d, h).wait_send()
            for d in range(1, depth_z):
                @pl.when(has(kind, d))
                def _(kind=kind, d=d):
                    y_forward(kind, d, h, lambda copy: copy.wait_send())

    each(0, pieces, sent)

    def extra_sent(h):
        for kind in idents:
            @pl.when(jnp.logical_not(from_partner(kind)))
            def _(kind=kind):
                extra_copy(kind, h).wait_send()

    each(late, pieces, extra_sent)
    swap.wait_send()
    for copy in row_copies:
        copy.wait_send()


def fused(rows, cols, panel, tiles, tile_slot, tile_col, pole_weight, box_orbitals, box_basis, supernode_basis):
    blocks, parts, shard_rows, width = panel.shape[1:]
    tile_count, _, block, _ = tiles.shape
    boxes, orbs = box_orbitals.shape
    points = box_basis.shape[2]
    half = block // cols
    peers = rows * cols
    capacity = 2 * boxes * orbs // peers
    depth_z = rows // 2
    pieces = blocks // 2
    dma = pltpu.SemaphoreType.DMA
    bf16, f32 = jnp.bfloat16, jnp.float32
    smem = pl.BlockSpec(memory_space=pltpu.SMEM)
    hbm = pl.BlockSpec(memory_space=pl.ANY)
    vmem = pl.BlockSpec(memory_space=pltpu.VMEM)
    return pl.pallas_call(
        functools.partial(kernel, rows, cols),
        name="pole_step",
        out_shape=(
            jax.ShapeDtypeStruct((BR_DEV, 2, half, width), f32),
            jax.ShapeDtypeStruct((boxes, points), f32),
        ),
        in_specs=[smem] * 3 + [hbm] * 5,
        out_specs=(vmem, vmem),
        scratch_shapes=[pltpu.VMEM((2, blocks, parts, shard_rows, width), bf16)] * (2 * depth_z - 1) + [
            pltpu.VMEM(tiles.shape, bf16),
            pltpu.VMEM(box_basis.shape, bf16),
            pltpu.VMEM(supernode_basis.shape, bf16),
            pltpu.VMEM((peers, boxes, orbs), jnp.int32),
            pltpu.VMEM((BR_DEV, block, 2 * width), f32),
            pltpu.VMEM((BR_DEV, half, 2 * width), f32),
            pltpu.VMEM((peers * capacity, BR_DEV * half), bf16),
            pltpu.VMEM((boxes, peers * capacity, points), bf16),
            pltpu.VMEM((peers, capacity, width), bf16),
            pltpu.VMEM((peers, capacity, width), bf16),
            dma((5,)),
            dma((2, depth_z, pieces)),
            dma((2, depth_z, pieces)),
            dma((2 * depth_z - 1, pieces)),
            dma((2 * depth_z - 1, pieces)),
            dma((pieces,)),
            dma((pieces,)),
            dma((2,)),
            dma((peers,)),
            dma((peers,)),
            dma((peers,)),
            dma((peers,)),
        ],
        compiler_params=pltpu.CompilerParams(
            collective_id=0, has_side_effects=True, vmem_limit_bytes=56 * 1024 * 1024),
    )(tile_slot, tile_col, pole_weight, panel, tiles, box_orbitals, box_basis, supernode_basis)


def plain(panel, tiles, tile_slot, tile_col, pole_weight, box_orbitals, box_basis, supernode_basis):
    gathered = lax.all_gather(panel, "row", axis=3, tiled=True)
    blocks = gathered[0]
    selector = (tile_col[:, None] == jnp.arange(blocks.shape[0], dtype=jnp.int32)[None, :]).astype(
        jnp.bfloat16
    )
    chosen = jnp.einsum(
        "tj,jcbs->tcbs", selector, blocks, preferred_element_type=jnp.float32
    ).astype(jnp.bfloat16)
    real_part = jnp.einsum(
        "tab,tbs->tas", tiles[:, 0], chosen[:, 0], preferred_element_type=jnp.float32
    )
    real_part = real_part - jnp.einsum(
        "tab,tbs->tas", tiles[:, 1], chosen[:, 1], preferred_element_type=jnp.float32
    )
    imag_part = jnp.einsum(
        "tab,tbs->tas", tiles[:, 0], chosen[:, 1], preferred_element_type=jnp.float32
    )
    imag_part = imag_part + jnp.einsum(
        "tab,tbs->tas", tiles[:, 1], chosen[:, 0], preferred_element_type=jnp.float32
    )
    products = jnp.stack([real_part, imag_part], axis=1)
    partial_value = jnp.stack(
        [
            jnp.sum(jnp.where((tile_slot == slot_row)[:, None, None, None], products, 0.0), axis=0)
            for slot_row in range(BR_DEV)
        ]
    )
    summed = lax.psum_scatter(partial_value, "col", scatter_dimension=2, tiled=True)
    inverse_column = -summed
    density_local = (
        pole_weight[0] * inverse_column[:, 1] + pole_weight[1] * inverse_column[:, 0]
    ).astype(jnp.bfloat16)
    columns = density_local.shape[2]
    density_local = density_local.reshape(-1, columns)
    block_width = tiles.shape[2]
    col_count = lax.axis_size("col")
    half_rows = block_width // col_count
    wanted = box_orbitals.reshape(-1)
    wanted_total = wanted.shape[0]
    block_index = wanted // block_width
    within = wanted % block_width
    source = block_index // BR_DEV * col_count + within // half_rows
    local_row = block_index % BR_DEV * half_rows + within % half_rows
    start_rows = jnp.zeros((wanted_total, columns), jnp.bfloat16)
    shards = lax.all_gather(density_local[None], ("row", "col"), axis=0, tiled=True)
    count = shards.shape[0]
    inside = (source >= 0) & (source < count)
    clipped = jnp.clip(source, 0, count - 1)
    fetched = shards[clipped, local_row]
    picked = jnp.where(inside[:, None], fetched, start_rows)
    picked = picked.reshape(box_basis.shape[0], box_basis.shape[1], columns)
    projected = jnp.einsum("nas,nap->nsp", picked, box_basis, preferred_element_type=jnp.float32)
    density = jnp.sum(supernode_basis.astype(jnp.float32) * projected, axis=1)
    return (inverse_column, density)


def solution(mesh):
    rows, cols = mesh.shape["row"], mesh.shape["col"]

    def local(panel, *rest):
        if cols == 2 and rows % 4 == 0 and panel.shape[1] % 4 == 0 and 2 * panel.shape[3] % panel.shape[4] == 0:
            return fused(rows, cols, panel, *rest)
        return plain(panel, *rest)

    return jax.shard_map(
        local,
        mesh=mesh,
        in_specs=(
            P(("pole", "col"), None, None, "row", None),
            P(("pole", "row", "col"), None, None, None),
            P(("pole", "row", "col")),
            P(("pole", "row", "col")),
            P("pole"),
            P(("pole", "row", "col"), None),
            P(("pole", "row", "col"), None, None),
            P(("pole", "row", "col"), None, None),
        ),
        out_specs=(P(("pole", "row"), None, "col", None), P(("pole", "row", "col"), None)),
        check_vma=False,
    )
```

profile of v0, /device:TPU:0, one launch (start us, length us, event | category | flops | bytes accessed | tf_op | source)
XLA Modules:
  0.0 46.9 jit_solution(907170100978962256)
XLA Ops:
  0.6 43.1 %pole_step.1 = (f32[2,2,256,128]{3,2,1,0:T(8,128)}, f32[2,512]{1,0:T(2,128)}) custom-call(s32[11]{0:T(128)} %slot_ref.1, s32[11]{0:T(128)} %tcol_ref.1, f32[2]{0:T(128)} %weight_ref.1, bf16[1,8,2,64,128]{4,3,2,1,0:T(8,128)(2,1)} %panel.1, bf16[11,2,512,512]{3,2,1,0:T(8,128)(2,1)} %tiles.1, s32[2,256]{1,0:T(2,128)} %orbitals.1, bf16[2,256,512]{2,1,0:T(8,128)(2,1)} %basis.1, ...), custom_call_target="tpu_custom_call" | custom-call | tf_op jit(solution)/shard_map/pole_step/pallas_call | solution.py:431
  43.8 1.9 %copy.12 = f32[2,2,256,128]{3,2,1,0:T(8,128)} copy(f32[2,2,256,128]{3,2,1,0:T(8,128)} %get-tuple-element.4) | data formatting | bytes 1048576
  45.6 1.3 %copy.13 = f32[2,512]{1,0:T(2,128)} copy(f32[2,512]{1,0:T(2,128)} %get-tuple-element.5) | data formatting | bytes 8192
where the time goes:
time: 47.7 us; the launch traced here: 46.9 us
  Pallas kernels  43.1 us (90%)
  local copies, waits for them, and re-layouts  3.14 us (7%)
  between operations  0.64 us (1%)
    pallas_call x1, Pallas kernels, fused(): pl.pallas_call(functools.partial(kernel, rows, cols), name='pole_step', o...  43.1 us
    unnamed x2, local copies, waits for them, and re-layouts  3.14 us

commit v1 on v0

v1 whole, which is shorter than its diff:
```python
import functools

import jax
import jax.numpy as jnp
from jax import lax
from jax.experimental import pallas as pl
from jax.experimental.pallas import tpu as pltpu
from jax.sharding import PartitionSpec as P

BR_DEV = 2
MESH = pl.DeviceIdType.MESH


def log2(value):
    assert value & (value - 1) == 0
    return value.bit_length() - 1


def kernel(
    rows, cols, slot_ref, tcol_ref, weight_ref, panel, tiles, orbitals, basis, super_basis,
    inv_ref, density_ref, own, near, third, last,
    tile_buf, basis_buf, super_buf, orb_buf, acc, half_in, pick_hot, basis_hot, order_buf, local_buf,
    send_rows, recv_rows, local_sem, send_sem, recv_sem, token, col_sem, orb_send, orb_recv, row_send, row_recv,
):
    lanes_y = 2
    depth_z = rows // lanes_y
    peers = rows * cols
    r = lax.axis_index("row")
    c = lax.axis_index("col")
    me = r * cols + c
    z = r // lanes_y
    y = r % lanes_y
    shard_rows = panel.shape[3]
    width = panel.shape[4]
    pieces = panel.shape[1]
    split_at = pieces // 2
    tile_count = tiles.shape[0]
    block = tiles.shape[2]
    half = block // cols
    pair = lanes_y * shard_rows
    boxes, orbs = orbitals.shape
    capacity = send_rows.shape[1]

    inner = 1 - 2 * (z // (depth_z // 2))
    corner = jnp.logical_or(z == 0, z == depth_z - 1)
    middle = jnp.logical_not(corner)
    other = r + 1 - 2 * y
    inward = r + lanes_y * inner
    outward = r - lanes_y * inner
    buffers = (own, near, third, last)
    places = (
        z,
        z + inner,
        jnp.where(corner, z + 2 * inner, z - inner),
        jnp.where(corner, z + 3 * inner, z + 2 * inner),
    )
    IN, OUT, Y = 0, 1, 2

    def spot(index):
        return {"row": index // cols, "col": index % cols}

    loads = [
        pltpu.make_async_copy(panel.at[0], own.at[y], local_sem.at[0]),
        pltpu.make_async_copy(orbitals, orb_buf.at[me], local_sem.at[4]),
        pltpu.make_async_copy(basis, basis_buf, local_sem.at[2]),
        pltpu.make_async_copy(tiles, tile_buf, local_sem.at[1]),
        pltpu.make_async_copy(super_basis, super_buf, local_sem.at[3]),
    ]
    for load in loads:
        load.start()

    barrier = pltpu.get_barrier_semaphore()
    for device in (
        {"row": other}, {"col": 1 - c}, {"row": other, "col": 1 - c}, {"row": inward},
    ):
        pl.semaphore_signal(barrier, inc=1, device_id=device, device_id_type=MESH)

    @pl.when(middle)
    def _():
        pl.semaphore_signal(barrier, inc=1, device_id={"row": outward}, device_id_type=MESH)
        pl.semaphore_wait(barrier, 5)

    @pl.when(corner)
    def _():
        pl.semaphore_wait(barrier, 4)

    def copy(link, kind, source, target, lane, p):
        row = (inward, outward, other)[link]
        src = panel.at[0, p] if source is None else buffers[source].at[lane, p]
        return pltpu.make_async_remote_copy(
            src_ref=src, dst_ref=buffers[target].at[lane, p],
            send_sem=send_sem.at[link, kind, p], recv_sem=recv_sem.at[target, lane, p],
            device_id={"row": row}, device_id_type=MESH,
        )

    def arrived(target, lane, p):
        dst = buffers[target].at[lane, p]
        pltpu.make_async_remote_copy(
            src_ref=dst, dst_ref=dst, send_sem=send_sem.at[0, 0, p], recv_sem=recv_sem.at[target, lane, p],
            device_id={"row": other}, device_id_type=MESH,
        ).wait_recv()

    def each(low, high, body):
        def run(h, carry):
            body(h)
            return carry
        lax.fori_loop(low, high, run, 0)

    corner_sends = {
        "own_in": (IN, 0, None, 2, y), "own_y": (Y, 0, None, 0, y),
        "extra": (IN, 1, 0, 2, 1 - y),
        "near_y": (Y, 1, 1, 1, y), "third_y": (Y, 2, 2, 2, y), "last_y": (Y, 3, 3, 3, y),
    }
    middle_sends = {
        "own_out": (OUT, 0, None, 1, y), "own_in": (IN, 0, None, 1, y), "own_y": (Y, 0, None, 0, y),
        "third_in": (IN, 1, 2, 3, y),
        "near_out": (OUT, 1, 1, 2, y), "near_y": (Y, 1, 1, 1, y),
        "last_out": (OUT, 2, 3, 3, y), "last_y": (Y, 2, 3, 3, y),
        "extra": (OUT, 3, 3, 3, 1 - y),
    }

    def at_corner(name, p):
        return copy(*corner_sends[name], p)

    def at_middle(name, p):
        return copy(*middle_sends[name], p)

    @pl.when(corner)
    def _():
        def go(p):
            at_corner("own_in", p).start()
            at_corner("own_y", p).start()
        each(0, pieces, go)

    @pl.when(middle)
    def _():
        def go(p):
            at_middle("own_out", p).start()
            at_middle("own_in", p).start()
            at_middle("own_y", p).start()
        each(0, pieces, go)

    acc[...] = jnp.zeros_like(acc)
    block_bits, half_bits = log2(block), log2(half)

    def split(g):
        row_block = g >> block_bits
        within = g & (block - 1)
        source = (row_block >> log2(BR_DEV)) * cols + (within >> half_bits)
        local = (row_block & (BR_DEV - 1)) * half + (within & (half - 1))
        return source, local

    def ranks(masks):
        before = lax.broadcasted_iota(jnp.int32, (orbs, orbs), 0)
        after = lax.broadcasted_iota(jnp.int32, (orbs, orbs), 1)
        upper = jnp.where(before <= after, 1.0, 0.0).astype(jnp.bfloat16)
        seen = jnp.zeros((masks[0].shape[0], 1), jnp.float32)
        result = []
        for mask in masks:
            counted = jnp.dot(mask.astype(jnp.bfloat16), upper, preferred_element_type=jnp.float32)
            result.append(counted - 1.0 + seen)
            seen = seen + jnp.sum(mask, axis=1, keepdims=True)
        return result

    def place_basis():
        loads[1].wait()
        loads[2].wait()
        masks = []
        peer_id = lax.broadcasted_iota(jnp.int32, (peers, orbs), 0)
        for n in range(boxes):
            source, _ = split(orb_buf[me, n:n + 1, :])
            masks.append(jnp.where(peer_id == source, 1.0, 0.0))
        order = ranks(masks)
        arrive = lax.broadcasted_iota(jnp.int32, (peers * capacity, orbs), 0).astype(jnp.float32)
        for n in range(boxes):
            position = jnp.sum(
                masks[n] * (order[n] + (peer_id * capacity).astype(jnp.float32)), axis=0, keepdims=True)
            hot = jnp.where(arrive == position, 1.0, 0.0).astype(jnp.bfloat16)
            basis_hot[n] = jnp.dot(hot, basis_buf[n], preferred_element_type=jnp.float32).astype(jnp.bfloat16)

    def orb_copy(k):
        return pltpu.make_async_remote_copy(
            src_ref=orbitals, dst_ref=orb_buf.at[me], send_sem=orb_send.at[k], recv_sem=orb_recv.at[k],
            device_id=spot((me + k) % peers), device_id_type=MESH,
        )

    def rank_orbitals():
        for k in range(1, peers):
            origin = (me + peers - k) % peers
            dst = orb_buf.at[origin]
            pltpu.make_async_remote_copy(
                src_ref=dst, dst_ref=dst, send_sem=orb_send.at[k], recv_sem=orb_recv.at[k],
                device_id=spot(origin), device_id_type=MESH,
            ).wait_recv()
        asked = []
        for n in range(boxes):
            g = jnp.concatenate([orb_buf[q, n:n + 1, :] for q in range(peers)], axis=0)
            source, local = split(g)
            asked.append((jnp.where(source == me, 1.0, 0.0), local.astype(jnp.float32)))
        order = ranks([a[0] for a in asked])
        for n in range(boxes):
            order_buf[n] = jnp.where(asked[n][0] > 0.5, order[n], -1.0)
            local_buf[n] = asked[n][1] + 1.0

    def place_picks(q):
        place = lax.broadcasted_iota(jnp.int32, (capacity, orbs), 0).astype(jnp.float32)
        row_id = lax.broadcasted_iota(jnp.int32, (capacity, BR_DEV * half), 1).astype(jnp.float32)
        found = jnp.zeros((capacity, 1), jnp.float32)
        for n in range(boxes):
            hit = place == order_buf[n, pl.ds(q, 1), :]
            found = found + jnp.sum(jnp.where(hit, local_buf[n, pl.ds(q, 1), :], 0.0), axis=1, keepdims=True)
        spot_rows = pl.ds(pl.multiple_of(q * capacity, capacity), capacity)
        pick_hot[spot_rows, :] = jnp.where(row_id == found - 1.0, 1.0, 0.0).astype(jnp.bfloat16)

    def product(which, t, out_rows):
        j = tcol_ref[t]
        offset = pl.multiple_of(places[which] * pair, pair)
        left = jnp.concatenate(
            [tile_buf[t, 0, out_rows, pl.ds(offset, pair)], tile_buf[t, 1, out_rows, pl.ds(offset, pair)]], axis=1)
        parts = [buffers[which][k, j] for k in range(lanes_y)]
        real = jnp.concatenate([p[0] for p in parts], axis=0)
        imag = jnp.concatenate([p[1] for p in parts], axis=0)
        right = jnp.concatenate(
            [jnp.concatenate([real, imag], axis=1), jnp.concatenate([-imag, real], axis=1)], axis=0)
        return jnp.dot(left, right, preferred_element_type=jnp.float32)

    def several(which, start, count, out_rows):
        values = [product(which, start + k, out_rows) for k in range(count)]
        for s in range(BR_DEV):
            total = jnp.where(slot_ref[start] == s, values[0], 0.0)
            for k in range(1, count):
                total = total + jnp.where(slot_ref[start + k] == s, values[k], 0.0)
            acc[s, out_rows, :] += total

    everything = pl.ds(0, block)

    def share(which, p):
        each(p * tile_count // pieces, (p + 1) * tile_count // pieces, lambda t: several(which, t, 1, everything))

    place_basis()

    def first(p):
        @pl.when(corner)
        def _():
            arrived(1, y, p)
            at_corner("near_y", p).start()
            arrived(0, 1 - y, p)
            at_corner("extra", p).start()

        @pl.when(middle)
        def _():
            arrived(2, y, p)
            at_middle("third_in", p).start()
            arrived(1, y, p)
            at_middle("near_out", p).start()
            at_middle("near_y", p).start()

            @pl.when(p == 0)
            def _():
                pl.semaphore_signal(token.at[0], inc=1, device_id={"row": inward}, device_id_type=MESH)

            @pl.when(p == pieces - 1)
            def _():
                pl.semaphore_wait(token.at[0], 1)
                pl.semaphore_signal(token.at[1], inc=1, device_id={"row": outward}, device_id_type=MESH)

    each(0, pieces, first)

    @pl.when(corner)
    def _():
        pl.semaphore_wait(token.at[1], 1)

    for k in range(1, peers):
        orb_copy(k).start()

    @pl.when(middle)
    def _():
        each(0, pieces, lambda p: arrived(0, 1 - y, p))

    loads[0].wait()
    loads[3].wait()

    def second(p):
        @pl.when(corner)
        def _():
            arrived(2, y, p)
            at_corner("third_y", p).start()

        @pl.when(middle)
        def _():
            arrived(3, y, p)
            at_middle("last_out", p).start()
            at_middle("last_y", p).start()

        share(0, p)

    each(0, pieces, second)
    each(0, pieces, lambda p: arrived(1, 1 - y, p))
    per = peers // (pieces - split_at)

    def closing(p):
        @pl.when(corner)
        def _():
            arrived(3, y, p)

            @pl.when(p >= split_at)
            def _():
                at_corner("last_y", p).start()

        @pl.when(jnp.logical_and(middle, p < split_at))
        def _():
            arrived(3, 1 - y, p)
            at_middle("extra", p).start()

        share(1, p)

        @pl.when(p == split_at - 1)
        def _():
            rank_orbitals()

        @pl.when(p >= split_at)
        def _():
            each((p - split_at) * per, (p - split_at + 1) * per, place_picks)

    each(0, pieces, closing)
    each(0, pieces, lambda p: arrived(2, 1 - y, p))
    for start in range(0, tile_count, 4):
        several(2, start, min(4, tile_count - start), everything)

    @pl.when(corner)
    def _():
        each(0, split_at, lambda p: arrived(3, 1 - y, p))
    each(split_at, pieces, lambda p: arrived(3, 1 - y, p))

    mine = pl.ds(pl.multiple_of(c * half, half), half)
    theirs = pl.ds(pl.multiple_of((1 - c) * half, half), half)
    for start in range(0, tile_count, 4):
        several(3, start, min(4, tile_count - start), theirs)
    swap = pltpu.make_async_remote_copy(
        src_ref=acc.at[:, theirs, :], dst_ref=half_in, send_sem=col_sem.at[0], recv_sem=col_sem.at[1],
        device_id={"col": 1 - c}, device_id_type=MESH,
    )
    swap.start()
    for start in range(0, tile_count, 4):
        several(3, start, min(4, tile_count - start), mine)
    swap.wait_recv()
    density_rows = []
    for s in range(BR_DEV):
        column = -(acc[s, mine, :] + half_in[s])
        real, imag = column[:, :width], column[:, width:]
        density_rows.append((weight_ref[0] * imag + weight_ref[1] * real).astype(jnp.bfloat16))
    density_rows = jnp.concatenate(density_rows, axis=0)

    group = lanes_y * cols

    def row_copy(target):
        return pltpu.make_async_remote_copy(
            src_ref=send_rows.at[target], dst_ref=recv_rows.at[me],
            send_sem=row_send.at[target], recv_sem=row_recv.at[me],
            device_id=spot(target), device_id_type=MESH,
        )

    for at_z in (places[3], places[2], places[1]):
        base = at_z * group
        hot = pick_hot[pl.ds(pl.multiple_of(base * capacity, group * capacity), group * capacity), :]
        picked = jnp.dot(hot, density_rows, preferred_element_type=jnp.float32).astype(jnp.bfloat16)
        send_rows[pl.ds(base, group)] = picked.reshape(group, capacity, width)
        for k in range(group):
            row_copy(base + k).start()
    base = z * group
    hot = pick_hot[pl.ds(pl.multiple_of(base * capacity, group * capacity), group * capacity), :]
    picked = jnp.dot(hot, density_rows, preferred_element_type=jnp.float32).astype(jnp.bfloat16)
    send_rows[pl.ds(base, group)] = picked.reshape(group, capacity, width)
    for k in range(1, group):
        row_copy(base + (me - base + k) % group).start()
    recv_rows[me] = send_rows[me]
    for s in range(BR_DEV):
        column = -(acc[s, mine, :] + half_in[s])
        inv_ref[s, 0] = column[:, :width]
        inv_ref[s, 1] = column[:, width:]
    loads[4].wait()
    for k in range(1, peers):
        origin = (me + k) % peers
        dst = recv_rows.at[origin]
        pltpu.make_async_remote_copy(
            src_ref=dst, dst_ref=dst, send_sem=row_send.at[origin], recv_sem=row_recv.at[origin],
            device_id=spot(origin), device_id_type=MESH,
        ).wait_recv()
    got = recv_rows[...].reshape(peers * capacity, width)
    for n in range(boxes):
        projected = lax.dot_general(
            got, basis_hot[n], (((0,), (0,)), ((), ())), preferred_element_type=jnp.float32)
        density_ref[n:n + 1, :] = jnp.sum(
            super_buf[n].astype(jnp.float32) * projected, axis=0, keepdims=True)

    @pl.when(corner)
    def _():
        def sent(p):
            for name in corner_sends:
                if name != "last_y":
                    at_corner(name, p).wait_send()
        each(0, pieces, sent)
        each(split_at, pieces, lambda p: at_corner("last_y", p).wait_send())

    @pl.when(middle)
    def _():
        def sent(p):
            for name in middle_sends:
                if name != "extra":
                    at_middle(name, p).wait_send()
        each(0, pieces, sent)
        each(0, split_at, lambda p: at_middle("extra", p).wait_send())

    swap.wait_send()
    for k in range(1, peers):
        orb_copy(k).wait_send()
        row_copy((me + k) % peers).wait_send()


def fused(rows, cols, panel, tiles, tile_slot, tile_col, pole_weight, box_orbitals, box_basis, supernode_basis):
    blocks, parts, shard_rows, width = panel.shape[1:]
    tile_count, _, block, _ = tiles.shape
    boxes, orbs = box_orbitals.shape
    points = box_basis.shape[2]
    half = block // cols
    peers = rows * cols
    capacity = 2 * boxes * orbs // peers
    dma = pltpu.SemaphoreType.DMA
    bf16, f32 = jnp.bfloat16, jnp.float32
    smem = pl.BlockSpec(memory_space=pltpu.SMEM)
    hbm = pl.BlockSpec(memory_space=pl.ANY)
    vmem = pl.BlockSpec(memory_space=pltpu.VMEM)
    return pl.pallas_call(
        functools.partial(kernel, rows, cols),
        name="pole_step",
        out_shape=(
            jax.ShapeDtypeStruct((BR_DEV, 2, half, width), f32),
            jax.ShapeDtypeStruct((boxes, points), f32),
        ),
        in_specs=[smem] * 3 + [hbm] * 5,
        out_specs=(vmem, vmem),
        scratch_shapes=[pltpu.VMEM((2, blocks, parts, shard_rows, width), bf16)] * 4 + [
            pltpu.VMEM(tiles.shape, bf16),
            pltpu.VMEM(box_basis.shape, bf16),
            pltpu.VMEM(supernode_basis.shape, bf16),
            pltpu.VMEM((peers, boxes, orbs), jnp.int32),
            pltpu.VMEM((BR_DEV, block, 2 * width), f32),
            pltpu.VMEM((BR_DEV, half, 2 * width), f32),
            pltpu.VMEM((peers * capacity, BR_DEV * half), bf16),
            pltpu.VMEM((boxes, peers * capacity, points), bf16),
            pltpu.VMEM((boxes, peers, orbs), f32),
            pltpu.VMEM((boxes, peers, orbs), f32),
            pltpu.VMEM((peers, capacity, width), bf16),
            pltpu.VMEM((peers, capacity, width), bf16),
            dma((5,)),
            dma((3, 4, blocks)),
            dma((4, 2, blocks)),
            pltpu.SemaphoreType.REGULAR((2,)),
            dma((2,)),
            dma((peers,)),
            dma((peers,)),
            dma((peers,)),
            dma((peers,)),
        ],
        compiler_params=pltpu.CompilerParams(
            collective_id=0, has_side_effects=True, vmem_limit_bytes=56 * 1024 * 1024),
    )(tile_slot, tile_col, pole_weight, panel, tiles, box_orbitals, box_basis, supernode_basis)


def plain(panel, tiles, tile_slot, tile_col, pole_weight, box_orbitals, box_basis, supernode_basis):
    gathered = lax.all_gather(panel, "row", axis=3, tiled=True)
    blocks = gathered[0]
    selector = (tile_col[:, None] == jnp.arange(blocks.shape[0], dtype=jnp.int32)[None, :]).astype(
        jnp.bfloat16
    )
    chosen = jnp.einsum(
        "tj,jcbs->tcbs", selector, blocks, preferred_element_type=jnp.float32
    ).astype(jnp.bfloat16)
    real_part = jnp.einsum(
        "tab,tbs->tas", tiles[:, 0], chosen[:, 0], preferred_element_type=jnp.float32
    )
    real_part = real_part - jnp.einsum(
        "tab,tbs->tas", tiles[:, 1], chosen[:, 1], preferred_element_type=jnp.float32
    )
    imag_part = jnp.einsum(
        "tab,tbs->tas", tiles[:, 0], chosen[:, 1], preferred_element_type=jnp.float32
    )
    imag_part = imag_part + jnp.einsum(
        "tab,tbs->tas", tiles[:, 1], chosen[:, 0], preferred_element_type=jnp.float32
    )
    products = jnp.stack([real_part, imag_part], axis=1)
    partial_value = jnp.stack(
        [
            jnp.sum(jnp.where((tile_slot == slot_row)[:, None, None, None], products, 0.0), axis=0)
            for slot_row in range(BR_DEV)
        ]
    )
    summed = lax.psum_scatter(partial_value, "col", scatter_dimension=2, tiled=True)
    inverse_column = -summed
    density_local = (
        pole_weight[0] * inverse_column[:, 1] + pole_weight[1] * inverse_column[:, 0]
    ).astype(jnp.bfloat16)
    columns = density_local.shape[2]
    density_local = density_local.reshape(-1, columns)
    block_width = tiles.shape[2]
    col_count = lax.axis_size("col")
    half_rows = block_width // col_count
    wanted = box_orbitals.reshape(-1)
    wanted_total = wanted.shape[0]
    block_index = wanted // block_width
    within = wanted % block_width
    source = block_index // BR_DEV * col_count + within // half_rows
    local_row = block_index % BR_DEV * half_rows + within % half_rows
    start_rows = jnp.zeros((wanted_total, columns), jnp.bfloat16)
    shards = lax.all_gather(density_local[None], ("row", "col"), axis=0, tiled=True)
    count = shards.shape[0]
    inside = (source >= 0) & (source < count)
    clipped = jnp.clip(source, 0, count - 1)
    fetched = shards[clipped, local_row]
    picked = jnp.where(inside[:, None], fetched, start_rows)
    picked = picked.reshape(box_basis.shape[0], box_basis.shape[1], columns)
    projected = jnp.einsum("nas,nap->nsp", picked, box_basis, preferred_element_type=jnp.float32)
    density = jnp.sum(supernode_basis.astype(jnp.float32) * projected, axis=1)
    return (inverse_column, density)


def solution(mesh):
    rows, cols = mesh.shape["row"], mesh.shape["col"]

    def local(panel, *rest):
        if cols == 2 and rows == 8 and panel.shape[1] % 8 == 0 and 2 * panel.shape[3] % panel.shape[4] == 0:
            return fused(rows, cols, panel, *rest)
        return plain(panel, *rest)

    return jax.shard_map(
        local,
        mesh=mesh,
        in_specs=(
            P(("pole", "col"), None, None, "row", None),
            P(("pole", "row", "col"), None, None, None),
            P(("pole", "row", "col")),
            P(("pole", "row", "col")),
            P("pole"),
            P(("pole", "row", "col"), None),
            P(("pole", "row", "col"), None, None),
            P(("pole", "row", "col"), None, None),
        ),
        out_specs=(P(("pole", "row"), None, "col", None), P(("pole", "row", "col"), None)),
        check_vma=False,
    )
```

time: 47.7 us -> 42.9 us (0.90)
  Pallas kernels: 43.1 us -> 38.3 us
    pallas_call x1, Pallas kernels: 43.1 us -> 38.3 us  [fused(): pl.pallas_call(functools.partial(kernel, rows, cols), name='pole_step', o...]
where the time goes in v1:
time: 42.9 us; the launch traced here: 42.1 us
  Pallas kernels  38.3 us (89%)
  local copies, waits for them, and re-layouts  3.14 us (7%)
  between operations  0.64 us (1%)
    pallas_call x1, Pallas kernels, fused(): pl.pallas_call(functools.partial(kernel, rows, cols), name='pole_step', o...  38.3 us
    unnamed x2, local copies, waits for them, and re-layouts  3.14 us

profile of v1, /device:TPU:0, one launch (start us, length us, event | category | flops | bytes accessed | tf_op | source)
XLA Modules:
  0.0 42.1 jit_solution(1612537899431853860)
XLA Ops:
  0.6 38.3 %pole_step.1 = (f32[2,2,256,128]{3,2,1,0:T(8,128)}, f32[2,512]{1,0:T(2,128)}) custom-call(s32[11]{0:T(128)} %slot_ref.1, s32[11]{0:T(128)} %tcol_ref.1, f32[2]{0:T(128)} %weight_ref.1, bf16[1,8,2,64,128]{4,3,2,1,0:T(8,128)(2,1)} %panel.1, bf16[11,2,512,512]{3,2,1,0:T(8,128)(2,1)} %tiles.1, s32[2,256]{1,0:T(2,128)} %orbitals.1, bf16[2,256,512]{2,1,0:T(8,128)(2,1)} %basis.1, ...), custom_call_target="tpu_custom_call" | custom-call | tf_op jit(solution)/shard_map/pole_step/pallas_call | solution.py:433
  38.9 1.9 %copy.12 = f32[2,2,256,128]{3,2,1,0:T(8,128)} copy(f32[2,2,256,128]{3,2,1,0:T(8,128)} %get-tuple-element.4) | data formatting | bytes 1048576
  40.8 1.3 %copy.13 = f32[2,512]{1,0:T(2,128)} copy(f32[2,512]{1,0:T(2,128)} %get-tuple-element.5) | data formatting | bytes 8192

commit v2 on v1

--- a/solution.py
+++ b/solution.py
@@ -32,7 +32,8 @@
     y = r % lanes_y
     shard_rows = panel.shape[3]
     width = panel.shape[4]
-    pieces = panel.shape[1]
+    pieces = recv_sem.shape[2]
+    step = panel.shape[1] // pieces
     split_at = pieces // 2
     tile_count = tiles.shape[0]
     block = tiles.shape[2]
@@ -66,7 +67,7 @@
         pltpu.make_async_copy(tiles, tile_buf, local_sem.at[1]),
         pltpu.make_async_copy(super_basis, super_buf, local_sem.at[3]),
     ]
-    for load in loads:
+    for load in loads[:3]:
         load.start()
 
     barrier = pltpu.get_barrier_semaphore()
@@ -84,17 +85,21 @@
     def _():
         pl.semaphore_wait(barrier, 4)
 
+    loads[0].wait()
+
+    def piece(which, lane, p):
+        return buffers[which].at[lane, pl.ds(p * step, step)]
+
     def copy(link, kind, source, target, lane, p):
         row = (inward, outward, other)[link]
-        src = panel.at[0, p] if source is None else buffers[source].at[lane, p]
         return pltpu.make_async_remote_copy(
-            src_ref=src, dst_ref=buffers[target].at[lane, p],
+            src_ref=piece(source, lane, p), dst_ref=piece(target, lane, p),
             send_sem=send_sem.at[link, kind, p], recv_sem=recv_sem.at[target, lane, p],
             device_id={"row": row}, device_id_type=MESH,
         )
 
     def arrived(target, lane, p):
-        dst = buffers[target].at[lane, p]
+        dst = piece(target, lane, p)
         pltpu.make_async_remote_copy(
             src_ref=dst, dst_ref=dst, send_sem=send_sem.at[0, 0, p], recv_sem=recv_sem.at[target, lane, p],
             device_id={"row": other}, device_id_type=MESH,
@@ -107,12 +112,12 @@
         lax.fori_loop(low, high, run, 0)
 
     corner_sends = {
-        "own_in": (IN, 0, None, 2, y), "own_y": (Y, 0, None, 0, y),
+        "own_in": (IN, 0, 0, 2, y), "own_y": (Y, 0, 0, 0, y),
         "extra": (IN, 1, 0, 2, 1 - y),
         "near_y": (Y, 1, 1, 1, y), "third_y": (Y, 2, 2, 2, y), "last_y": (Y, 3, 3, 3, y),
     }
     middle_sends = {
-        "own_out": (OUT, 0, None, 1, y), "own_in": (IN, 0, None, 1, y), "own_y": (Y, 0, None, 0, y),
+        "own_out": (OUT, 0, 0, 1, y), "own_in": (IN, 0, 0, 1, y), "own_y": (Y, 0, 0, 0, y),
         "third_in": (IN, 1, 2, 3, y),
         "near_out": (OUT, 1, 1, 2, y), "near_y": (Y, 1, 1, 1, y),
         "last_out": (OUT, 2, 3, 3, y), "last_y": (Y, 2, 3, 3, y),
@@ -140,6 +145,8 @@
             at_middle("own_y", p).start()
         each(0, pieces, go)
 
+    for load in loads[3:]:
+        load.start()
     acc[...] = jnp.zeros_like(acc)
     block_bits, half_bits = log2(block), log2(half)
 
@@ -234,8 +241,8 @@
 
     everything = pl.ds(0, block)
 
-    def share(which, p):
-        each(p * tile_count // pieces, (p + 1) * tile_count // pieces, lambda t: several(which, t, 1, everything))
+    def share(which, p, parts):
+        each(p * tile_count // parts, (p + 1) * tile_count // parts, lambda t: several(which, t, 1, everything))
 
     place_basis()
 
@@ -277,7 +284,6 @@
     def _():
         each(0, pieces, lambda p: arrived(0, 1 - y, p))
 
-    loads[0].wait()
     loads[3].wait()
 
     def second(p):
@@ -290,47 +296,46 @@
         def _():
             arrived(3, y, p)
             at_middle("last_out", p).start()
-            at_middle("last_y", p).start()
-
-        share(0, p)
+
+            @pl.when(p >= split_at)
+            def _():
+                at_middle("last_y", p).start()
+
+        share(0, p, pieces)
 
     each(0, pieces, second)
+
+    @pl.when(middle)
+    def _():
+        each(0, split_at, lambda p: at_middle("last_y", p).start())
+
     each(0, pieces, lambda p: arrived(1, 1 - y, p))
-    per = peers // (pieces - split_at)
 
     def closing(p):
+        share(1, p, split_at)
+
         @pl.when(corner)
         def _():
             arrived(3, y, p)
-
-            @pl.when(p >= split_at)
-            def _():
-                at_corner("last_y", p).start()
-
-        @pl.when(jnp.logical_and(middle, p < split_at))
+            at_corner("last_y", p).start()
+
+        @pl.when(middle)
         def _():
-            arrived(3, 1 - y, p)
-            at_middle("extra", p).start()
-
-        share(1, p)
-
-        @pl.when(p == split_at - 1)
-        def _():
-            rank_orbitals()
-
-        @pl.when(p >= split_at)
-        def _():
-            each((p - split_at) * per, (p - split_at + 1) * per, place_picks)
-
-    each(0, pieces, closing)
+            arrived(3, 1 - y, p + split_at)
+            at_middle("extra", p + split_at).start()
+
+    each(0, split_at, closing)
+    rank_orbitals()
+    each(0, peers, place_picks)
     each(0, pieces, lambda p: arrived(2, 1 - y, p))
     for start in range(0, tile_count, 4):
         several(2, start, min(4, tile_count - start), everything)
 
     @pl.when(corner)
     def _():
-        each(0, split_at, lambda p: arrived(3, 1 - y, p))
-    each(split_at, pieces, lambda p: arrived(3, 1 - y, p))
+        each(split_at, pieces, lambda p: arrived(3, y, p))
+        each(split_at, pieces, lambda p: arrived(3, 1 - y, p))
+    each(0, split_at, lambda p: arrived(3, 1 - y, p))
 
     mine = pl.ds(pl.multiple_of(c * half, half), half)
     theirs = pl.ds(pl.multiple_of((1 - c) * half, half), half)
@@ -400,7 +405,7 @@
                 if name != "last_y":
                     at_corner(name, p).wait_send()
         each(0, pieces, sent)
-        each(split_at, pieces, lambda p: at_corner("last_y", p).wait_send())
+        each(0, split_at, lambda p: at_corner("last_y", p).wait_send())
 
     @pl.when(middle)
     def _():
@@ -409,7 +414,7 @@
                 if name != "extra":
                     at_middle(name, p).wait_send()
         each(0, pieces, sent)
-        each(0, split_at, lambda p: at_middle("extra", p).wait_send())
+        each(split_at, pieces, lambda p: at_middle("extra", p).wait_send())
 
     swap.wait_send()
     for k in range(1, peers):
@@ -425,6 +430,7 @@
     half = block // cols
     peers = rows * cols
     capacity = 2 * boxes * orbs // peers
+    pieces = blocks // 2
     dma = pltpu.SemaphoreType.DMA
     bf16, f32 = jnp.bfloat16, jnp.float32
     smem = pl.BlockSpec(memory_space=pltpu.SMEM)
@@ -453,8 +459,8 @@
             pltpu.VMEM((peers, capacity, width), bf16),
             pltpu.VMEM((peers, capacity, width), bf16),
             dma((5,)),
-            dma((3, 4, blocks)),
-            dma((4, 2, blocks)),
+            dma((3, 4, pieces)),
+            dma((4, 2, pieces)),
             pltpu.SemaphoreType.REGULAR((2,)),
             dma((2,)),
             dma((peers,)),

time: 42.9 us -> 40.6 us (0.946); the launches traced: 42.1 us -> 40.4 us
  Pallas kernels: 38.3 us -> 36.6 us
    pallas_call x1, Pallas kernels: 38.3 us -> 36.6 us  [fused(): pl.pallas_call(functools.partial(kernel, rows, cols), name='pole_step', o...]
where the time goes in v2:
time: 40.6 us; the launch traced here: 40.4 us
  Pallas kernels  36.6 us (90%)
  local copies, waits for them, and re-layouts  3.14 us (8%)
  between operations  0.64 us (2%)
    pallas_call x1, Pallas kernels, fused(): pl.pallas_call(functools.partial(kernel, rows, cols), name='pole_step', o...  36.6 us
    unnamed x2, local copies, waits for them, and re-layouts  3.14 us

profile of v2, /device:TPU:0, one launch (start us, length us, event | category | flops | bytes accessed | tf_op | source)
XLA Modules:
  0.0 40.4 jit_solution(2629015235839358785)
XLA Ops:
  0.6 36.6 %pole_step.1 = (f32[2,2,256,128]{3,2,1,0:T(8,128)}, f32[2,512]{1,0:T(2,128)}) custom-call(s32[11]{0:T(128)} %slot_ref.1, s32[11]{0:T(128)} %tcol_ref.1, f32[2]{0:T(128)} %weight_ref.1, bf16[1,8,2,64,128]{4,3,2,1,0:T(8,128)(2,1)} %panel.1, bf16[11,2,512,512]{3,2,1,0:T(8,128)(2,1)} %tiles.1, s32[2,256]{1,0:T(2,128)} %orbitals.1, bf16[2,256,512]{2,1,0:T(8,128)(2,1)} %basis.1, ...), custom_call_target="tpu_custom_call" | custom-call | tf_op jit(solution)/shard_map/pole_step/pallas_call | solution.py:439
  37.3 1.9 %copy.12 = f32[2,2,256,128]{3,2,1,0:T(8,128)} copy(f32[2,2,256,128]{3,2,1,0:T(8,128)} %get-tuple-element.4) | data formatting | bytes 1048576
  39.1 1.3 %copy.13 = f32[2,512]{1,0:T(2,128)} copy(f32[2,512]{1,0:T(2,128)} %get-tuple-element.5) | data formatting | bytes 8192

commit v3 on v2

--- a/solution.py
+++ b/solution.py
@@ -422,6 +422,17 @@
         row_copy((me + k) % peers).wait_send()
 
 
+def deliver(column, density, column_out, density_out, sem):
+    copies = [
+        pltpu.make_async_copy(column, column_out, sem.at[0]),
+        pltpu.make_async_copy(density, density_out, sem.at[1]),
+    ]
+    for copy in copies:
+        copy.start()
+    for copy in copies:
+        copy.wait()
+
+
 def fused(rows, cols, panel, tiles, tile_slot, tile_col, pole_weight, box_orbitals, box_basis, supernode_basis):
     blocks, parts, shard_rows, width = panel.shape[1:]
     tile_count, _, block, _ = tiles.shape
@@ -436,12 +447,12 @@
     smem = pl.BlockSpec(memory_space=pltpu.SMEM)
     hbm = pl.BlockSpec(memory_space=pl.ANY)
     vmem = pl.BlockSpec(memory_space=pltpu.VMEM)
-    return pl.pallas_call(
+    column, density = pl.pallas_call(
         functools.partial(kernel, rows, cols),
         name="pole_step",
         out_shape=(
-            jax.ShapeDtypeStruct((BR_DEV, 2, half, width), f32),
-            jax.ShapeDtypeStruct((boxes, points), f32),
+            pltpu.VMEM((BR_DEV, 2, half, width), f32),
+            pltpu.VMEM((boxes, points), f32),
         ),
         in_specs=[smem] * 3 + [hbm] * 5,
         out_specs=(vmem, vmem),
@@ -471,6 +482,18 @@
         compiler_params=pltpu.CompilerParams(
             collective_id=0, has_side_effects=True, vmem_limit_bytes=56 * 1024 * 1024),
     )(tile_slot, tile_col, pole_weight, panel, tiles, box_orbitals, box_basis, supernode_basis)
+    return pl.pallas_call(
+        deliver,
+        name="deliver",
+        out_shape=(
+            jax.ShapeDtypeStruct(column.shape, f32),
+            jax.ShapeDtypeStruct(density.shape, f32),
+        ),
+        in_specs=[vmem] * 2,
+        out_specs=(hbm, hbm),
+        scratch_shapes=[dma((2,))],
+        compiler_params=pltpu.CompilerParams(vmem_limit_bytes=8 * 1024 * 1024),
+    )(column, density)
 
 
 def plain(panel, tiles, tile_slot, tile_col, pole_weight, box_orbitals, box_basis, supernode_basis):

time: 40.6 us -> 37.5 us (0.924)
  local copies, waits for them, and re-layouts: 3.14 us -> 0 us
    unnamed x2 -> x0, local copies, waits for them, and re-layouts: 3.14 us -> none
    pallas_call x0 -> x1, Pallas kernels: none -> 0.81 us  [fused(): pl.pallas_call(deliver, name='deliver', out_shape=(jax.ShapeDtypeStruct(c...]
    pallas_call x1, Pallas kernels: 36.6 us -> 35.8 us  [fused(): pl.pallas_call(functools.partial(kernel, rows, cols), name='pole_step', o...]
where the time goes in v3:
time: 37.5 us; the launch traced here: 37.3 us
  Pallas kernels  36.6 us (98%)
  between operations  0.64 us (2%)
    pallas_call x1, Pallas kernels, fused(): pl.pallas_call(functools.partial(kernel, rows, cols), name='pole_step', o...  35.8 us
    pallas_call x1, Pallas kernels, fused(): pl.pallas_call(deliver, name='deliver', out_shape=(jax.ShapeDtypeStruct(c...  0.81 us

profile of v3, /device:TPU:0, one launch (start us, length us, event | category | flops | bytes accessed | tf_op | source)
XLA Modules:
  0.0 37.3 jit_solution(16488435007066831170)
XLA Ops:
  0.6 35.8 %pole_step.1 = (f32[2,2,256,128]{3,2,1,0:T(8,128)S(1)}, f32[2,512]{1,0:T(2,128)S(1)}) custom-call(s32[11]{0:T(128)} %slot_ref.1, s32[11]{0:T(128)} %tcol_ref.1, f32[2]{0:T(128)} %weight_ref.1, bf16[1,8,2,64,128]{4,3,2,1,0:T(8,128)(2,1)} %panel.1, bf16[11,2,512,512]{3,2,1,0:T(8,128)(2,1)} %tiles.1, s32[2,256]{1,0:T(2,128)} %orbitals.1, ...), custom_call_target="tpu_custom_call" | custom-call | tf_op jit(solution)/shard_map/pole_step/pallas_call | solution.py:450
  36.5 0.8 %deliver.1 = (f32[2,2,256,128]{3,2,1,0:T(8,128)}, f32[2,512]{1,0:T(2,128)}) custom-call(f32[2,2,256,128]{3,2,1,0:T(8,128)S(1)} %get-tuple-element.4.column, f32[2,512]{1,0:T(2,128)S(1)} %get-tuple-element.5.density), custom_call_target="tpu_custom_call" | custom-call | tf_op jit(solution)/shard_map/deliver/pallas_call | solution.py:485

commit v4 on v3

--- a/solution.py
+++ b/solution.py
@@ -19,7 +19,7 @@
 def kernel(
     rows, cols, slot_ref, tcol_ref, weight_ref, panel, tiles, orbitals, basis, super_basis,
     inv_ref, density_ref, own, near, third, last,
-    tile_buf, basis_buf, super_buf, orb_buf, acc, half_in, pick_hot, basis_hot, order_buf, local_buf,
+    tile_buf, basis_buf, super_buf, orb_buf, acc, half_in, mix_out, mix_own, mix_in, pick_hot, basis_hot, order_buf, local_buf,
     send_rows, recv_rows, local_sem, send_sem, recv_sem, token, col_sem, orb_send, orb_recv, row_send, row_recv,
 ):
     lanes_y = 2
@@ -242,7 +242,9 @@
     everything = pl.ds(0, block)
 
     def share(which, p, parts):
-        each(p * tile_count // parts, (p + 1) * tile_count // parts, lambda t: several(which, t, 1, everything))
+        first_tile, last_tile = p * tile_count // parts, (p + 1) * tile_count // parts
+        for start in range(first_tile, last_tile, 4):
+            several(which, start, min(4, last_tile - start), everything)
 
     place_basis()
 
@@ -296,14 +298,13 @@
         def _():
             arrived(3, y, p)
             at_middle("last_out", p).start()
-
-            @pl.when(p >= split_at)
-            def _():
+            if p >= split_at:
                 at_middle("last_y", p).start()
 
         share(0, p, pieces)
 
-    each(0, pieces, second)
+    for p in range(pieces):
+        second(p)
 
     @pl.when(middle)
     def _():
@@ -324,12 +325,12 @@
             arrived(3, 1 - y, p + split_at)
             at_middle("extra", p + split_at).start()
 
-    each(0, split_at, closing)
+    for p in range(split_at):
+        closing(p)
     rank_orbitals()
-    each(0, peers, place_picks)
+    each(0, peers // 4, lambda q: [place_picks(4 * q + k) for k in range(4)])
     each(0, pieces, lambda p: arrived(2, 1 - y, p))
-    for start in range(0, tile_count, 4):
-        several(2, start, min(4, tile_count - start), everything)
+    share(2, 0, 1)
 
     @pl.when(corner)
     def _():
@@ -339,21 +340,31 @@
 
     mine = pl.ds(pl.multiple_of(c * half, half), half)
     theirs = pl.ds(pl.multiple_of((1 - c) * half, half), half)
+
+    def to_partner(which, src, dst):
+        return pltpu.make_async_remote_copy(
+            src_ref=src, dst_ref=dst, send_sem=col_sem.at[0, which], recv_sem=col_sem.at[1, which],
+            device_id={"col": 1 - c}, device_id_type=MESH,
+        )
+
+    mix_swap = to_partner(0, mix_out, mix_in)
+    swap = to_partner(1, acc.at[:, theirs, :], half_in)
+
+    def mixed(s, out_rows):
+        return weight_ref[0] * acc[s, out_rows, width:] + weight_ref[1] * acc[s, out_rows, :width]
+
     for start in range(0, tile_count, 4):
         several(3, start, min(4, tile_count - start), theirs)
-    swap = pltpu.make_async_remote_copy(
-        src_ref=acc.at[:, theirs, :], dst_ref=half_in, send_sem=col_sem.at[0], recv_sem=col_sem.at[1],
-        device_id={"col": 1 - c}, device_id_type=MESH,
-    )
+    for s in range(BR_DEV):
+        mix_out[s] = mixed(s, theirs)
+    mix_swap.start()
     swap.start()
     for start in range(0, tile_count, 4):
         several(3, start, min(4, tile_count - start), mine)
-    swap.wait_recv()
-    density_rows = []
     for s in range(BR_DEV):
-        column = -(acc[s, mine, :] + half_in[s])
-        real, imag = column[:, :width], column[:, width:]
-        density_rows.append((weight_ref[0] * imag + weight_ref[1] * real).astype(jnp.bfloat16))
+        mix_own[s] = mixed(s, mine)
+    mix_swap.wait_recv()
+    density_rows = [(-(mix_own[s] + mix_in[s])).astype(jnp.bfloat16) for s in range(BR_DEV)]
     density_rows = jnp.concatenate(density_rows, axis=0)
 
     group = lanes_y * cols
@@ -379,24 +390,12 @@
     for k in range(1, group):
         row_copy(base + (me - base + k) % group).start()
     recv_rows[me] = send_rows[me]
+    swap.wait_recv()
     for s in range(BR_DEV):
         column = -(acc[s, mine, :] + half_in[s])
         inv_ref[s, 0] = column[:, :width]
         inv_ref[s, 1] = column[:, width:]
     loads[4].wait()
-    for k in range(1, peers):
-        origin = (me + k) % peers
-        dst = recv_rows.at[origin]
-        pltpu.make_async_remote_copy(
-            src_ref=dst, dst_ref=dst, send_sem=row_send.at[origin], recv_sem=row_recv.at[origin],
-            device_id=spot(origin), device_id_type=MESH,
-        ).wait_recv()
-    got = recv_rows[...].reshape(peers * capacity, width)
-    for n in range(boxes):
-        projected = lax.dot_general(
-            got, basis_hot[n], (((0,), (0,)), ((), ())), preferred_element_type=jnp.float32)
-        density_ref[n:n + 1, :] = jnp.sum(
-            super_buf[n].astype(jnp.float32) * projected, axis=0, keepdims=True)
 
     @pl.when(corner)
     def _():
@@ -416,10 +415,33 @@
         each(0, pieces, sent)
         each(split_at, pieces, lambda p: at_middle("extra", p).wait_send())
 
+    mix_swap.wait_send()
     swap.wait_send()
     for k in range(1, peers):
         orb_copy(k).wait_send()
-        row_copy((me + k) % peers).wait_send()
+
+    projected = [None] * boxes
+    for at_z in range(depth_z):
+        if at_z == depth_z - 1:
+            for k in range(1, peers):
+                row_copy((me + k) % peers).wait_send()
+        for origin in range(at_z * group, (at_z + 1) * group):
+            @pl.when(me != origin)
+            def _(origin=origin):
+                dst = recv_rows.at[origin]
+                pltpu.make_async_remote_copy(
+                    src_ref=dst, dst_ref=dst, send_sem=row_send.at[origin], recv_sem=row_recv.at[origin],
+                    device_id={"row": other}, device_id_type=MESH,
+                ).wait_recv()
+        got = recv_rows[at_z * group:(at_z + 1) * group].reshape(group * capacity, width)
+        for n in range(boxes):
+            value = lax.dot_general(
+                got, basis_hot[n, at_z * group * capacity:(at_z + 1) * group * capacity, :],
+                (((0,), (0,)), ((), ())), preferred_element_type=jnp.float32)
+            projected[n] = value if at_z == 0 else projected[n] + value
+    for n in range(boxes):
+        density_ref[n:n + 1, :] = jnp.sum(
+            super_buf[n].astype(jnp.float32) * projected[n], axis=0, keepdims=True)
 
 
 def deliver(column, density, column_out, density_out, sem):
@@ -463,6 +485,9 @@
             pltpu.VMEM((peers, boxes, orbs), jnp.int32),
             pltpu.VMEM((BR_DEV, block, 2 * width), f32),
             pltpu.VMEM((BR_DEV, half, 2 * width), f32),
+            pltpu.VMEM((BR_DEV, half, width), f32),
+            pltpu.VMEM((BR_DEV, half, width), f32),
+            pltpu.VMEM((BR_DEV, half, width), f32),
             pltpu.VMEM((peers * capacity, BR_DEV * half), bf16),
             pltpu.VMEM((boxes, peers * capacity, points), bf16),
             pltpu.VMEM((boxes, peers, orbs), f32),
@@ -473,7 +498,7 @@
             dma((3, 4, pieces)),
             dma((4, 2, pieces)),
             pltpu.SemaphoreType.REGULAR((2,)),
-            dma((2,)),
+            dma((2, 2)),
             dma((peers,)),
             dma((peers,)),
             dma((peers,)),

time: 37.5 us -> 36.9 us (0.984)
  Pallas kernels: 36.6 us -> 35.9 us
    pallas_call x1, Pallas kernels: 35.8 us -> 35.1 us  [fused(): pl.pallas_call(functools.partial(kernel, rows, cols), name='pole_step', o...]
where the time goes in v4:
time: 36.9 us; the launch traced here: 36.6 us
  Pallas kernels  35.9 us (97%)
  between operations  0.64 us (2%)
    pallas_call x1, Pallas kernels, fused(): pl.pallas_call(functools.partial(kernel, rows, cols), name='pole_step', o...  35.1 us
    pallas_call x1, Pallas kernels, fused(): pl.pallas_call(deliver, name='deliver', out_shape=(jax.ShapeDtypeStruct(c...  0.81 us

profile of v4, /device:TPU:0, one launch (start us, length us, event | category | flops | bytes accessed | tf_op | source)
XLA Modules:
  0.0 36.6 jit_solution(11515262008351434776)
XLA Ops:
  0.6 35.1 %pole_step.1 = (f32[2,2,256,128]{3,2,1,0:T(8,128)S(1)}, f32[2,512]{1,0:T(2,128)S(1)}) custom-call(s32[11]{0:T(128)} %slot_ref.1, s32[11]{0:T(128)} %tcol_ref.1, f32[2]{0:T(128)} %weight_ref.1, bf16[1,8,2,64,128]{4,3,2,1,0:T(8,128)(2,1)} %panel.1, bf16[11,2,512,512]{3,2,1,0:T(8,128)(2,1)} %tiles.1, s32[2,256]{1,0:T(2,128)} %orbitals.1, ...), custom_call_target="tpu_custom_call" | custom-call | tf_op jit(solution)/shard_map/pole_step/pallas_call | solution.py:472
  35.8 0.8 %deliver.1 = (f32[2,2,256,128]{3,2,1,0:T(8,128)}, f32[2,512]{1,0:T(2,128)}) custom-call(f32[2,2,256,128]{3,2,1,0:T(8,128)S(1)} %get-tuple-element.4.column, f32[2,512]{1,0:T(2,128)S(1)} %get-tuple-element.5.density), custom_call_target="tpu_custom_call" | custom-call | tf_op jit(solution)/shard_map/deliver/pallas_call | solution.py:510

commit v5 on v4

--- a/solution.py
+++ b/solution.py
@@ -17,8 +17,8 @@
 
 
 def kernel(
-    rows, cols, slot_ref, tcol_ref, weight_ref, panel, tiles, orbitals, basis, super_basis,
-    inv_ref, density_ref, own, near, third, last,
+    rows, cols, slots, tile_cols, weights, panel, tiles, orbitals, basis, super_basis,
+    inv_ref, density_ref, slot_ref, tcol_ref, weight_ref, own, near, third, last,
     tile_buf, basis_buf, super_buf, orb_buf, acc, half_in, mix_out, mix_own, mix_in, pick_hot, basis_hot, order_buf, local_buf,
     send_rows, recv_rows, local_sem, send_sem, recv_sem, token, col_sem, orb_send, orb_recv, row_send, row_recv,
 ):
@@ -66,10 +66,10 @@
         pltpu.make_async_copy(basis, basis_buf, local_sem.at[2]),
         pltpu.make_async_copy(tiles, tile_buf, local_sem.at[1]),
         pltpu.make_async_copy(super_basis, super_buf, local_sem.at[3]),
+        pltpu.make_async_copy(slots, slot_ref, local_sem.at[5]),
+        pltpu.make_async_copy(tile_cols, tcol_ref, local_sem.at[6]),
+        pltpu.make_async_copy(weights, weight_ref, local_sem.at[7]),
     ]
-    for load in loads[:3]:
-        load.start()
-
     barrier = pltpu.get_barrier_semaphore()
     for device in (
         {"row": other}, {"col": 1 - c}, {"row": other, "col": 1 - c}, {"row": inward},
@@ -79,6 +79,12 @@
     @pl.when(middle)
     def _():
         pl.semaphore_signal(barrier, inc=1, device_id={"row": outward}, device_id_type=MESH)
+
+    for load in loads[:3]:
+        load.start()
+
+    @pl.when(middle)
+    def _():
         pl.semaphore_wait(barrier, 5)
 
     @pl.when(corner)
@@ -287,6 +293,8 @@
         each(0, pieces, lambda p: arrived(0, 1 - y, p))
 
     loads[3].wait()
+    for load in loads[5:]:
+        load.wait()
 
     def second(p):
         @pl.when(corner)
@@ -466,7 +474,6 @@
     pieces = blocks // 2
     dma = pltpu.SemaphoreType.DMA
     bf16, f32 = jnp.bfloat16, jnp.float32
-    smem = pl.BlockSpec(memory_space=pltpu.SMEM)
     hbm = pl.BlockSpec(memory_space=pl.ANY)
     vmem = pl.BlockSpec(memory_space=pltpu.VMEM)
     column, density = pl.pallas_call(
@@ -476,9 +483,13 @@
             pltpu.VMEM((BR_DEV, 2, half, width), f32),
             pltpu.VMEM((boxes, points), f32),
         ),
-        in_specs=[smem] * 3 + [hbm] * 5,
+        in_specs=[hbm] * 8,
         out_specs=(vmem, vmem),
-        scratch_shapes=[pltpu.VMEM((2, blocks, parts, shard_rows, width), bf16)] * 4 + [
+        scratch_shapes=[
+            pltpu.SMEM(tile_slot.shape, jnp.int32),
+            pltpu.SMEM(tile_col.shape, jnp.int32),
+            pltpu.SMEM(pole_weight.shape, f32),
+        ] + [pltpu.VMEM((2, blocks, parts, shard_rows, width), bf16)] * 4 + [
             pltpu.VMEM(tiles.shape, bf16),
             pltpu.VMEM(box_basis.shape, bf16),
             pltpu.VMEM(supernode_basis.shape, bf16),
@@ -494,7 +505,7 @@
             pltpu.VMEM((boxes, peers, orbs), f32),
             pltpu.VMEM((peers, capacity, width), bf16),
             pltpu.VMEM((peers, capacity, width), bf16),
-            dma((5,)),
+            dma((8,)),
             dma((3, 4, pieces)),
             dma((4, 2, pieces)),
             pltpu.SemaphoreType.REGULAR((2,)),

time: 36.9 us -> 36.2 us (0.981)
  Pallas kernels: 35.9 us -> 35.3 us
    pallas_call x1, Pallas kernels: 35.1 us -> 34.5 us  [fused(): pl.pallas_call(functools.partial(kernel, rows, cols), name='pole_step', o...]
where the time goes in v5:
time: 36.2 us; the launch traced here: 35.9 us
  Pallas kernels  35.3 us (98%)
  between operations  0.64 us (2%)
    pallas_call x1, Pallas kernels, fused(): pl.pallas_call(functools.partial(kernel, rows, cols), name='pole_step', o...  34.5 us
    pallas_call x1, Pallas kernels, fused(): pl.pallas_call(deliver, name='deliver', out_shape=(jax.ShapeDtypeStruct(c...  0.81 us

profile of v5, /device:TPU:0, one launch (start us, length us, event | category | flops | bytes accessed | tf_op | source)
XLA Modules:
  0.0 35.9 jit_solution(1282967983601373685)
XLA Ops:
  0.6 34.5 %pole_step.1 = (f32[2,2,256,128]{3,2,1,0:T(8,128)S(1)}, f32[2,512]{1,0:T(2,128)S(1)}) custom-call(s32[11]{0:T(128)} %slots.1, s32[11]{0:T(128)} %tile_cols.1, f32[2]{0:T(128)} %weights.1, bf16[1,8,2,64,128]{4,3,2,1,0:T(8,128)(2,1)} %panel.1, bf16[11,2,512,512]{3,2,1,0:T(8,128)(2,1)} %tiles.1, s32[2,256]{1,0:T(2,128)} %orbitals.1, ...), custom_call_target="tpu_custom_call" | custom-call | tf_op jit(solution)/shard_map/pole_step/pallas_call | solution.py:479
  35.1 0.8 %deliver.1 = (f32[2,2,256,128]{3,2,1,0:T(8,128)}, f32[2,512]{1,0:T(2,128)}) custom-call(f32[2,2,256,128]{3,2,1,0:T(8,128)S(1)} %get-tuple-element.4.column, f32[2,512]{1,0:T(2,128)S(1)} %get-tuple-element.5.density), custom_call_target="tpu_custom_call" | custom-call | tf_op jit(solution)/shard_map/deliver/pallas_call | solution.py:521

commit v6 on v5

--- a/solution.py
+++ b/solution.py
@@ -62,7 +62,7 @@
 
     loads = [
         pltpu.make_async_copy(panel.at[0], own.at[y], local_sem.at[0]),
-        pltpu.make_async_copy(orbitals, orb_buf.at[me], local_sem.at[4]),
+        pltpu.make_async_copy(orbitals, orb_buf.at[c, r], local_sem.at[4]),
         pltpu.make_async_copy(basis, basis_buf, local_sem.at[2]),
         pltpu.make_async_copy(tiles, tile_buf, local_sem.at[1]),
         pltpu.make_async_copy(super_basis, super_buf, local_sem.at[3]),
@@ -181,7 +181,7 @@
         masks = []
         peer_id = lax.broadcasted_iota(jnp.int32, (peers, orbs), 0)
         for n in range(boxes):
-            source, _ = split(orb_buf[me, n:n + 1, :])
+            source, _ = split(orb_buf[c, r, n:n + 1, :])
             masks.append(jnp.where(peer_id == source, 1.0, 0.0))
         order = ranks(masks)
         arrive = lax.broadcasted_iota(jnp.int32, (peers * capacity, orbs), 0).astype(jnp.float32)
@@ -193,21 +193,30 @@
 
     def orb_copy(k):
         return pltpu.make_async_remote_copy(
-            src_ref=orbitals, dst_ref=orb_buf.at[me], send_sem=orb_send.at[k], recv_sem=orb_recv.at[k],
-            device_id=spot((me + k) % peers), device_id_type=MESH,
+            src_ref=orbitals, dst_ref=orb_buf.at[c, r], send_sem=orb_send.at[k], recv_sem=orb_recv.at[k],
+            device_id={"row": (r + k) % rows}, device_id_type=MESH,
         )
 
-    def rank_orbitals():
-        for k in range(1, peers):
-            origin = (me + peers - k) % peers
-            dst = orb_buf.at[origin]
+    def orb_block(col):
+        return pltpu.make_async_remote_copy(
+            src_ref=orb_buf.at[col], dst_ref=orb_buf.at[col], send_sem=orb_send.at[0], recv_sem=orb_recv.at[0],
+            device_id={"col": 1 - c}, device_id_type=MESH,
+        )
+
+    def pass_orbitals():
+        for k in range(1, rows):
+            dst = orb_buf.at[c, (r + rows - k) % rows]
             pltpu.make_async_remote_copy(
                 src_ref=dst, dst_ref=dst, send_sem=orb_send.at[k], recv_sem=orb_recv.at[k],
-                device_id=spot(origin), device_id_type=MESH,
+                device_id={"row": other}, device_id_type=MESH,
             ).wait_recv()
+        orb_block(c).start()
+
+    def rank_orbitals():
+        orb_block(1 - c).wait_recv()
         asked = []
         for n in range(boxes):
-            g = jnp.concatenate([orb_buf[q, n:n + 1, :] for q in range(peers)], axis=0)
+            g = jnp.concatenate([orb_buf[q % cols, q // cols, n:n + 1, :] for q in range(peers)], axis=0)
             source, local = split(g)
             asked.append((jnp.where(source == me, 1.0, 0.0), local.astype(jnp.float32)))
         order = ranks([a[0] for a in asked])
@@ -285,7 +294,7 @@
     def _():
         pl.semaphore_wait(token.at[1], 1)
 
-    for k in range(1, peers):
+    for k in range(1, rows):
         orb_copy(k).start()
 
     @pl.when(middle)
@@ -335,10 +344,21 @@
 
     for p in range(split_at):
         closing(p)
+    pass_orbitals()
+
+    @pl.when(middle)
+    def _():
+        each(0, pieces, lambda p: arrived(2, 1 - y, p))
+        share(2, 0, 1)
+
     rank_orbitals()
     each(0, peers // 4, lambda q: [place_picks(4 * q + k) for k in range(4)])
-    each(0, pieces, lambda p: arrived(2, 1 - y, p))
-    share(2, 0, 1)
+
+    @pl.when(corner)
+    def _():
+        each(0, pieces, lambda p: arrived(2, 1 - y, p))
+        share(2, 0, 1)
+
 
     @pl.when(corner)
     def _():
@@ -384,13 +404,14 @@
             device_id=spot(target), device_id_type=MESH,
         )
 
-    for at_z in (places[3], places[2], places[1]):
+    for k in range(depth_z - 1):
+        at_z = k + jnp.where(k >= z, 1, 0)
         base = at_z * group
         hot = pick_hot[pl.ds(pl.multiple_of(base * capacity, group * capacity), group * capacity), :]
         picked = jnp.dot(hot, density_rows, preferred_element_type=jnp.float32).astype(jnp.bfloat16)
         send_rows[pl.ds(base, group)] = picked.reshape(group, capacity, width)
-        for k in range(group):
-            row_copy(base + k).start()
+        for lane in range(group):
+            row_copy(base + lane).start()
     base = z * group
     hot = pick_hot[pl.ds(pl.multiple_of(base * capacity, group * capacity), group * capacity), :]
     picked = jnp.dot(hot, density_rows, preferred_element_type=jnp.float32).astype(jnp.bfloat16)
@@ -425,8 +446,9 @@
 
     mix_swap.wait_send()
     swap.wait_send()
-    for k in range(1, peers):
+    for k in range(1, rows):
         orb_copy(k).wait_send()
+    orb_block(c).wait_send()
 
     projected = [None] * boxes
     for at_z in range(depth_z):
@@ -493,7 +515,7 @@
             pltpu.VMEM(tiles.shape, bf16),
             pltpu.VMEM(box_basis.shape, bf16),
             pltpu.VMEM(supernode_basis.shape, bf16),
-            pltpu.VMEM((peers, boxes, orbs), jnp.int32),
+            pltpu.VMEM((cols, rows, boxes, orbs), jnp.int32),
             pltpu.VMEM((BR_DEV, block, 2 * width), f32),
             pltpu.VMEM((BR_DEV, half, 2 * width), f32),
             pltpu.VMEM((BR_DEV, half, width), f32),

time: 36.2 us -> 35.8 us (0.989)
  no operation moved by 1% of the time
where the time goes in v6:
time: 35.8 us; the launch traced here: 35.6 us
  Pallas kernels  35 us (98%)
  between operations  0.64 us (2%)
    pallas_call x1, Pallas kernels, fused(): pl.pallas_call(functools.partial(kernel, rows, cols), name='pole_step', o...  34.2 us
    pallas_call x1, Pallas kernels, fused(): pl.pallas_call(deliver, name='deliver', out_shape=(jax.ShapeDtypeStruct(c...  0.81 us

profile of v6, /device:TPU:0, one launch (start us, length us, event | category | flops | bytes accessed | tf_op | source)
XLA Modules:
  0.0 35.6 jit_solution(14697576122008410538)
XLA Ops:
  0.6 34.2 %pole_step.1 = (f32[2,2,256,128]{3,2,1,0:T(8,128)S(1)}, f32[2,512]{1,0:T(2,128)S(1)}) custom-call(s32[11]{0:T(128)} %slots.1, s32[11]{0:T(128)} %tile_cols.1, f32[2]{0:T(128)} %weights.1, bf16[1,8,2,64,128]{4,3,2,1,0:T(8,128)(2,1)} %panel.1, bf16[11,2,512,512]{3,2,1,0:T(8,128)(2,1)} %tiles.1, s32[2,256]{1,0:T(2,128)} %orbitals.1, ...), custom_call_target="tpu_custom_call" | custom-call | tf_op jit(solution)/shard_map/pole_step/pallas_call | solution.py:501
  34.8 0.8 %deliver.1 = (f32[2,2,256,128]{3,2,1,0:T(8,128)}, f32[2,512]{1,0:T(2,128)}) custom-call(f32[2,2,256,128]{3,2,1,0:T(8,128)S(1)} %get-tuple-element.4.column, f32[2,512]{1,0:T(2,128)S(1)} %get-tuple-element.5.density), custom_call_target="tpu_custom_call" | custom-call | tf_op jit(solution)/shard_map/deliver/pallas_call | solution.py:543

commit v7 on v6

--- a/solution.py
+++ b/solution.py
@@ -18,8 +18,8 @@
 
 def kernel(
     rows, cols, slots, tile_cols, weights, panel, tiles, orbitals, basis, super_basis,
-    inv_ref, density_ref, slot_ref, tcol_ref, weight_ref, own, near, third, last,
-    tile_buf, basis_buf, super_buf, orb_buf, acc, half_in, mix_out, mix_own, mix_in, pick_hot, basis_hot, order_buf, local_buf,
+    inv_ref, projected_ref, late_rows, late_basis, super_buf, slot_ref, tcol_ref, weight_ref, own, near, third, last,
+    tile_buf, basis_buf, orb_buf, acc, half_in, mix_out, mix_own, mix_in, pick_hot, basis_hot, order_buf, local_buf,
     send_rows, recv_rows, local_sem, send_sem, recv_sem, token, col_sem, orb_send, orb_recv, row_send, row_recv,
 ):
     lanes_y = 2
@@ -189,7 +189,10 @@
             position = jnp.sum(
                 masks[n] * (order[n] + (peer_id * capacity).astype(jnp.float32)), axis=0, keepdims=True)
             hot = jnp.where(arrive == position, 1.0, 0.0).astype(jnp.bfloat16)
-            basis_hot[n] = jnp.dot(hot, basis_buf[n], preferred_element_type=jnp.float32).astype(jnp.bfloat16)
+            placed = jnp.dot(hot, basis_buf[n], preferred_element_type=jnp.float32).astype(jnp.bfloat16)
+            early = basis_hot.shape[1]
+            basis_hot[n] = placed[:early]
+            late_basis[n] = placed[early:]
 
     def orb_copy(k):
         return pltpu.make_async_remote_copy(
@@ -345,20 +348,10 @@
     for p in range(split_at):
         closing(p)
     pass_orbitals()
-
-    @pl.when(middle)
-    def _():
-        each(0, pieces, lambda p: arrived(2, 1 - y, p))
-        share(2, 0, 1)
-
+    each(0, pieces, lambda p: arrived(2, 1 - y, p))
+    share(2, 0, 1)
     rank_orbitals()
     each(0, peers // 4, lambda q: [place_picks(4 * q + k) for k in range(4)])
-
-    @pl.when(corner)
-    def _():
-        each(0, pieces, lambda p: arrived(2, 1 - y, p))
-        share(2, 0, 1)
-
 
     @pl.when(corner)
     def _():
@@ -405,13 +398,14 @@
         )
 
     for k in range(depth_z - 1):
-        at_z = k + jnp.where(k >= z, 1, 0)
-        base = at_z * group
-        hot = pick_hot[pl.ds(pl.multiple_of(base * capacity, group * capacity), group * capacity), :]
-        picked = jnp.dot(hot, density_rows, preferred_element_type=jnp.float32).astype(jnp.bfloat16)
-        send_rows[pl.ds(base, group)] = picked.reshape(group, capacity, width)
-        for lane in range(group):
-            row_copy(base + lane).start()
+        for part in range(lanes_y if k == 0 else 1):
+            count = cols if k == 0 else group
+            base = (k + jnp.where(k >= z, 1, 0)) * group + part * count
+            hot = pick_hot[pl.ds(pl.multiple_of(base * capacity, count * capacity), count * capacity), :]
+            picked = jnp.dot(hot, density_rows, preferred_element_type=jnp.float32).astype(jnp.bfloat16)
+            send_rows[pl.ds(base, count)] = picked.reshape(count, capacity, width)
+            for lane in range(count):
+                row_copy(base + lane).start()
     base = z * group
     hot = pick_hot[pl.ds(pl.multiple_of(base * capacity, group * capacity), group * capacity), :]
     picked = jnp.dot(hot, density_rows, preferred_element_type=jnp.float32).astype(jnp.bfloat16)
@@ -463,26 +457,33 @@
                     src_ref=dst, dst_ref=dst, send_sem=row_send.at[origin], recv_sem=row_recv.at[origin],
                     device_id={"row": other}, device_id_type=MESH,
                 ).wait_recv()
+        if at_z == depth_z - 1:
+            late_rows[...] = recv_rows[at_z * group:(at_z + 1) * group]
+            continue
         got = recv_rows[at_z * group:(at_z + 1) * group].reshape(group * capacity, width)
         for n in range(boxes):
             value = lax.dot_general(
                 got, basis_hot[n, at_z * group * capacity:(at_z + 1) * group * capacity, :],
                 (((0,), (0,)), ((), ())), preferred_element_type=jnp.float32)
             projected[n] = value if at_z == 0 else projected[n] + value
+        if at_z == depth_z - 2:
+            for n in range(boxes):
+                projected_ref[n] = projected[n]
+
+
+def deliver(column, projected, late_rows, late_basis, super_basis, column_out, density_out, density, sem):
+    column_copy = pltpu.make_async_copy(column, column_out, sem.at[0])
+    column_copy.start()
+    boxes, width, _ = projected.shape
+    got = late_rows[...].reshape(late_basis.shape[1], width)
     for n in range(boxes):
-        density_ref[n:n + 1, :] = jnp.sum(
-            super_buf[n].astype(jnp.float32) * projected[n], axis=0, keepdims=True)
-
-
-def deliver(column, density, column_out, density_out, sem):
-    copies = [
-        pltpu.make_async_copy(column, column_out, sem.at[0]),
-        pltpu.make_async_copy(density, density_out, sem.at[1]),
-    ]
-    for copy in copies:
-        copy.start()
-    for copy in copies:
-        copy.wait()
+        value = projected[n] + lax.dot_general(
+            got, late_basis[n], (((0,), (0,)), ((), ())), preferred_element_type=jnp.float32)
+        density[n:n + 1, :] = jnp.sum(super_basis[n].astype(jnp.float32) * value, axis=0, keepdims=True)
+    density_copy = pltpu.make_async_copy(density, density_out, sem.at[1])
+    density_copy.start()
+    density_copy.wait()
+    column_copy.wait()
 
 
 def fused(rows, cols, panel, tiles, tile_slot, tile_col, pole_weight, box_orbitals, box_basis, supernode_basis):
@@ -498,15 +499,19 @@
     bf16, f32 = jnp.bfloat16, jnp.float32
     hbm = pl.BlockSpec(memory_space=pl.ANY)
     vmem = pl.BlockSpec(memory_space=pltpu.VMEM)
-    column, density = pl.pallas_call(
+    late = 2 * cols * capacity
+    results = pl.pallas_call(
         functools.partial(kernel, rows, cols),
         name="pole_step",
         out_shape=(
             pltpu.VMEM((BR_DEV, 2, half, width), f32),
-            pltpu.VMEM((boxes, points), f32),
+            pltpu.VMEM((boxes, width, points), f32),
+            pltpu.VMEM((2 * cols, capacity, width), bf16),
+            pltpu.VMEM((boxes, late, points), bf16),
+            pltpu.VMEM(supernode_basis.shape, bf16),
         ),
         in_specs=[hbm] * 8,
-        out_specs=(vmem, vmem),
+        out_specs=(vmem,) * 5,
         scratch_shapes=[
             pltpu.SMEM(tile_slot.shape, jnp.int32),
             pltpu.SMEM(tile_col.shape, jnp.int32),
@@ -514,7 +519,6 @@
         ] + [pltpu.VMEM((2, blocks, parts, shard_rows, width), bf16)] * 4 + [
             pltpu.VMEM(tiles.shape, bf16),
             pltpu.VMEM(box_basis.shape, bf16),
-            pltpu.VMEM(supernode_basis.shape, bf16),
             pltpu.VMEM((cols, rows, boxes, orbs), jnp.int32),
             pltpu.VMEM((BR_DEV, block, 2 * width), f32),
             pltpu.VMEM((BR_DEV, half, 2 * width), f32),
@@ -522,7 +526,7 @@
             pltpu.VMEM((BR_DEV, half, width), f32),
             pltpu.VMEM((BR_DEV, half, width), f32),
             pltpu.VMEM((peers * capacity, BR_DEV * half), bf16),
-            pltpu.VMEM((boxes, peers * capacity, points), bf16),
+            pltpu.VMEM((boxes, peers * capacity - late, points), bf16),
             pltpu.VMEM((boxes, peers, orbs), f32),
             pltpu.VMEM((boxes, peers, orbs), f32),
             pltpu.VMEM((peers, capacity, width), bf16),
@@ -544,14 +548,14 @@
         deliver,
         name="deliver",
         out_shape=(
-            jax.ShapeDtypeStruct(column.shape, f32),
-            jax.ShapeDtypeStruct(density.shape, f32),
+            jax.ShapeDtypeStruct((BR_DEV, 2, half, width), f32),
+            jax.ShapeDtypeStruct((boxes, points), f32),
         ),
-        in_specs=[vmem] * 2,
+        in_specs=[vmem] * 5,
         out_specs=(hbm, hbm),
-        scratch_shapes=[dma((2,))],
+        scratch_shapes=[pltpu.VMEM((boxes, points), f32), dma((2,))],
         compiler_params=pltpu.CompilerParams(vmem_limit_bytes=8 * 1024 * 1024),
-    )(column, density)
+    )(*results)
 
 
 def plain(panel, tiles, tile_slot, tile_col, pole_weight, box_orbitals, box_basis, supernode_basis):

time: 35.8 us -> 35.6 us (level)
  no operation moved by 1% of the time
where the time goes in v7:
time: 35.6 us; the launch traced here: 35.4 us
  Pallas kernels  34.8 us (98%)
  between operations  0.64 us (2%)
    pallas_call x1, Pallas kernels, fused(): pl.pallas_call(functools.partial(kernel, rows, cols), name='pole_step', o...  33.9 us
    pallas_call x1, Pallas kernels, fused(): pl.pallas_call(deliver, name='deliver', out_shape=(jax.ShapeDtypeStruct((...  0.89 us

profile of v7, /device:TPU:0, one launch (start us, length us, event | category | flops | bytes accessed | tf_op | source)
XLA Modules:
  0.0 35.4 jit_solution(17236680316374185016)
XLA Ops:
  0.6 33.9 %pole_step.1 = (f32[2,2,256,128]{3,2,1,0:T(8,128)S(1)}, f32[2,128,512]{2,1,0:T(8,128)S(1)}, bf16[4,64,128]{2,1,0:T(8,128)(2,1)S(1)}, bf16[2,256,512]{2,1,0:T(8,128)(2,1)S(1)}, bf16[2,128,512]{2,1,0:T(8,128)(2,1)S(1)}) custom-call(s32[11]{0:T(128)} %slots.1, s32[11]{0:T(128)} %tile_cols.1, f32[2]{0:T(128)} %weights.1, bf16[1,8,2,64,128]{4,3,2,1,0:T(8,128)(2,1)} %panel.1, ...), custom_call_target="tpu_custom_call" | custom-call | tf_op jit(solution)/shard_map/pole_step/pallas_call | solution.py:503
  34.6 0.9 %deliver.1 = (f32[2,2,256,128]{3,2,1,0:T(8,128)}, f32[2,512]{1,0:T(2,128)}) custom-call(f32[2,2,256,128]{3,2,1,0:T(8,128)S(1)} %get-tuple-element.7.column, f32[2,128,512]{2,1,0:T(8,128)S(1)} %get-tuple-element.8.projected, bf16[4,64,128]{2,1,0:T(8,128)(2,1)S(1)} %get-tuple-element.9.late_rows, bf16[2,256,512]{2,1,0:T(8,128)(2,1)S(1)} %get-tuple-element.10.late_basis, ...), custom_call_target="tpu_custom_call" | custom-call | tf_op jit(solution)/shard_map/deliver/pallas_call | solution.py:547

commit v8 on v7

--- a/solution.py
+++ b/solution.py
@@ -379,7 +379,6 @@
     for s in range(BR_DEV):
         mix_out[s] = mixed(s, theirs)
     mix_swap.start()
-    swap.start()
     for start in range(0, tile_count, 4):
         several(3, start, min(4, tile_count - start), mine)
     for s in range(BR_DEV):
@@ -412,6 +411,7 @@
     send_rows[pl.ds(base, group)] = picked.reshape(group, capacity, width)
     for k in range(1, group):
         row_copy(base + (me - base + k) % group).start()
+    swap.start()
     recv_rows[me] = send_rows[me]
     swap.wait_recv()
     for s in range(BR_DEV):

time: 35.6 us -> 35.6 us (level)
  no operation moved by 1% of the time
where the time goes in v8:
time: 35.6 us; the launch traced here: 35.4 us
  Pallas kernels  34.8 us (98%)
  between operations  0.64 us (2%)
    pallas_call x1, Pallas kernels, fused(): pl.pallas_call(functools.partial(kernel, rows, cols), name='pole_step', o...  33.9 us
    pallas_call x1, Pallas kernels, fused(): pl.pallas_call(deliver, name='deliver', out_shape=(jax.ShapeDtypeStruct((...  0.88 us

profile of v8, /device:TPU:0, one launch (start us, length us, event | category | flops | bytes accessed | tf_op | source)
XLA Modules:
  0.0 35.4 jit_solution(7660830415979391446)
XLA Ops:
  0.6 33.9 %pole_step.1 = (f32[2,2,256,128]{3,2,1,0:T(8,128)S(1)}, f32[2,128,512]{2,1,0:T(8,128)S(1)}, bf16[4,64,128]{2,1,0:T(8,128)(2,1)S(1)}, bf16[2,256,512]{2,1,0:T(8,128)(2,1)S(1)}, bf16[2,128,512]{2,1,0:T(8,128)(2,1)S(1)}) custom-call(s32[11]{0:T(128)} %slots.1, s32[11]{0:T(128)} %tile_cols.1, f32[2]{0:T(128)} %weights.1, bf16[1,8,2,64,128]{4,3,2,1,0:T(8,128)(2,1)} %panel.1, ...), custom_call_target="tpu_custom_call" | custom-call | tf_op jit(solution)/shard_map/pole_step/pallas_call | solution.py:503
  34.6 0.9 %deliver.1 = (f32[2,2,256,128]{3,2,1,0:T(8,128)}, f32[2,512]{1,0:T(2,128)}) custom-call(f32[2,2,256,128]{3,2,1,0:T(8,128)S(1)} %get-tuple-element.7.column, f32[2,128,512]{2,1,0:T(8,128)S(1)} %get-tuple-element.8.projected, bf16[4,64,128]{2,1,0:T(8,128)(2,1)S(1)} %get-tuple-element.9.late_rows, bf16[2,256,512]{2,1,0:T(8,128)(2,1)S(1)} %get-tuple-element.10.late_basis, ...), custom_call_target="tpu_custom_call" | custom-call | tf_op jit(solution)/shard_map/deliver/pallas_call | solution.py:547

commit v9 on v8

--- a/solution.py
+++ b/solution.py
@@ -397,8 +397,8 @@
         )
 
     for k in range(depth_z - 1):
-        for part in range(lanes_y if k == 0 else 1):
-            count = cols if k == 0 else group
+        for part in range(lanes_y):
+            count = cols
             base = (k + jnp.where(k >= z, 1, 0)) * group + part * count
             hot = pick_hot[pl.ds(pl.multiple_of(base * capacity, count * capacity), count * capacity), :]
             picked = jnp.dot(hot, density_rows, preferred_element_type=jnp.float32).astype(jnp.bfloat16)

time: 35.6 us -> 35.6 us (level)
  no operation moved by 1% of the time
where the time goes in v9:
time: 35.6 us; the launch traced here: 35.4 us
  Pallas kernels  34.8 us (98%)
  between operations  0.64 us (2%)
    pallas_call x1, Pallas kernels, fused(): pl.pallas_call(functools.partial(kernel, rows, cols), name='pole_step', o...  33.9 us
    pallas_call x1, Pallas kernels, fused(): pl.pallas_call(deliver, name='deliver', out_shape=(jax.ShapeDtypeStruct((...  0.88 us

profile of v9, /device:TPU:0, one launch (start us, length us, event | category | flops | bytes accessed | tf_op | source)
XLA Modules:
  0.0 35.4 jit_solution(16737225670131015411)
XLA Ops:
  0.6 33.9 %pole_step.1 = (f32[2,2,256,128]{3,2,1,0:T(8,128)S(1)}, f32[2,128,512]{2,1,0:T(8,128)S(1)}, bf16[4,64,128]{2,1,0:T(8,128)(2,1)S(1)}, bf16[2,256,512]{2,1,0:T(8,128)(2,1)S(1)}, bf16[2,128,512]{2,1,0:T(8,128)(2,1)S(1)}) custom-call(s32[11]{0:T(128)} %slots.1, s32[11]{0:T(128)} %tile_cols.1, f32[2]{0:T(128)} %weights.1, bf16[1,8,2,64,128]{4,3,2,1,0:T(8,128)(2,1)} %panel.1, ...), custom_call_target="tpu_custom_call" | custom-call | tf_op jit(solution)/shard_map/pole_step/pallas_call | solution.py:503
  34.6 0.9 %deliver.1 = (f32[2,2,256,128]{3,2,1,0:T(8,128)}, f32[2,512]{1,0:T(2,128)}) custom-call(f32[2,2,256,128]{3,2,1,0:T(8,128)S(1)} %get-tuple-element.7.column, f32[2,128,512]{2,1,0:T(8,128)S(1)} %get-tuple-element.8.projected, bf16[4,64,128]{2,1,0:T(8,128)(2,1)S(1)} %get-tuple-element.9.late_rows, bf16[2,256,512]{2,1,0:T(8,128)(2,1)S(1)} %get-tuple-element.10.late_basis, ...), custom_call_target="tpu_custom_call" | custom-call | tf_op jit(solution)/shard_map/deliver/pallas_call | solution.py:547
